TPU v7x, 32 devices: a whole 2x2x4 slice. The times are simulated.
32 devices in a mesh: dp: 8 (over z, x), shard: 4 (over y, core).
Axes of the slice: x: 2, y: 2, z: 4, core: 2. Of those that a mesh axis runs over, the one named last changes fastest.
Arguments:
- inputs: bfloat16 [2, 8, 512, 1024], P(None, 'dp', 'shard'), may hold values from -6 to 6
- segments: int32 [2, 8, 512], P(None, 'dp', 'shard'), may hold values from 0 to 7, never falling along the last dimension, each value on 1 to 256 neighbouring positions
- padding: int32 [2, 8, 512], P(None, 'dp', 'shard'), may hold values 0 or 1
- routes_value: int32 [2, 8, 512, 4, 2], P(None, 'dp', 'shard'), may hold values from 0 to 4, all different within a row
- routes_output: int32 [2, 8, 512, 4, 2], P(None, 'dp', 'shard'), may hold values from 0 to 4, all different within a row
- norm1_gain: bfloat16 [1024], P('shard'), may hold values from 0.5 to 1.5
- norm1_bias: bfloat16 [1024], P('shard'), may hold values from -1.25 to 1.25
- query_weight: bfloat16 [1024, 448], P('shard'), may hold values from -0.1875 to 0.1875
- key_weight: bfloat16 [1024, 448], P('shard'), may hold values from -0.1875 to 0.1875
- pos_weight: bfloat16 [1024, 448], P('shard'), may hold values from -0.1875 to 0.1875
- content_bias: bfloat16 [448], P('shard'), may hold values from -3 to 3
- pos_bias: bfloat16 [448], P('shard'), may hold values from -3 to 3
- value_router: bfloat16 [1024, 20], P('shard'), may hold values from -0.1875 to 0.1875
- output_router: bfloat16 [1024, 20], P('shard'), may hold values from -0.1875 to 0.1875
- value_experts: bfloat16 [1024, 2240], P('shard'), may hold values from -0.1875 to 0.1875
- output_experts: bfloat16 [2240, 1024], P('shard'), may hold values from -3 to 3
- norm2_gain: bfloat16 [1024], P('shard'), may hold values from 0.5 to 1.5
- norm2_bias: bfloat16 [1024], P('shard'), may hold values from -1.25 to 1.25
- ffn_in: bfloat16 [1024, 4096], P('shard'), may hold values from -0.1875 to 0.1875
- ffn_in_bias: bfloat16 [4096], P('shard'), may hold values from -1.75 to 1.75
- ffn_out: bfloat16 [4096, 1024], P('shard'), may hold values from -0.125 to 0.125
- ffn_out_bias: bfloat16 [1024], P('shard'), may hold values from -1.75 to 1.75
- cotangent: bfloat16 [2, 8, 512, 1024], P(None, 'dp', 'shard'), may hold values from -6 to 6
Outputs:
- output: bfloat16 [2, 8, 512, 1024], P(None, 'dp', 'shard')
- input_grad: float32 [2, 8, 512, 1024], P(None, 'dp', 'shard')
- norm1_gain_grad: float32 [1024], P('shard')
- norm1_bias_grad: float32 [1024], P('shard')
- query_weight_grad: float32 [1024, 448], P('shard')
- key_weight_grad: float32 [1024, 448], P('shard')
- pos_weight_grad: float32 [1024, 448], P('shard')
- content_bias_grad: float32 [448], P('shard')
- pos_bias_grad: float32 [448], P('shard')
- value_router_grad: float32 [1024, 20], P('shard')
- output_router_grad: float32 [1024, 20], P('shard')
- value_experts_grad: float32 [1024, 2240], P('shard')
- output_experts_grad: float32 [2240, 1024], P('shard')
- norm2_gain_grad: float32 [1024], P('shard')
- norm2_bias_grad: float32 [1024], P('shard')
- ffn_in_grad: float32 [1024, 4096], P('shard')
- ffn_in_bias_grad: float32 [4096], P('shard')
- ffn_out_grad: float32 [4096, 1024], P('shard')
- ffn_out_bias_grad: float32 [1024], P('shard')
Inputs may be any that keep to these rules, and one draw needn't show every extreme that they name: `routes_value`: each token names 2 different value experts in each head. `routes_output`: each token names 2 different output experts in each head. `segments`: document numbers never fall along a sequence; a document has 1 to 256 tokens.
All inputs are finite; a program needn't handle non-finite values. No bound on the sum of `padding` on one device may be relied on, other than what follows from the above.
Results may differ from a plain program's by a relative error of at most 0.017.
Values may be sent and summed in bfloat16 or wider, within the bound.
No kernel may reach another device: no remote copies, remote signals or barrier semaphores. Data moves between devices by JAX's collectives and lax.ppermute only.
A program may use at most 192 MiB of HBM per device.

v0:
```python
import functools
import math

import jax
import jax.numpy as jnp
from jax import lax
from jax.experimental import pallas as pl
from jax.experimental.pallas import tpu as pltpu
from jax.sharding import PartitionSpec as P

D = 1024
H = 4
DH = 112
E = 5
FF = 4096
LANE = 128
PACK = 1024
BLK = 128
RING = 8
TAIL = 8
MASKED = -1e30
SCALE = DH ** (-0.5)
bf16 = jnp.bfloat16
f32 = jnp.float32
NN = (((1,), (0,)), ((), ()))
NT = (((1,), (1,)), ((), ()))
TN = (((0,), (0,)), ((), ()))


def mm(a, b, dims=NN):
    return lax.dot_general(a, b, dims, preferred_element_type=f32)


def call(kernel, outs, args, scratch=(), copies=0, flops=0, vmem=12, smem=2, deps=(), into=None):
    in_specs, arrays = [], []
    args = list(args)
    count = len(args)
    into = into or {}
    deps = [*deps, *into.values()]
    aliases = {count + len(deps) - len(into) + n: i for n, i in enumerate(into)}
    args += [Far(d, pl.ANY) for d in deps]
    body = lambda *refs: kernel(*refs[:count], *refs[count + len(deps) :])
    for i, arg in enumerate(args):
        far = isinstance(arg, Far)
        space = pltpu.SMEM if i < smem else arg.space if far else pltpu.VMEM
        in_specs.append(pl.BlockSpec(memory_space=space))
        arrays.append(arg.value if far else arg)
    out_specs, out_shapes = [], []
    for o in outs:
        far = isinstance(o, Far)
        out_specs.append(pl.BlockSpec(memory_space=o.space if far else pltpu.VMEM))
        out_shapes.append(o.value if far else o)
    moved = sum(math.prod(a.shape) * a.dtype.itemsize for a in arrays + out_shapes)
    scratch = list(scratch)
    if copies:
        scratch.append(pltpu.SemaphoreType.DMA((copies,)))
    return pl.pallas_call(
        body if deps else kernel,
        out_shape=out_shapes,
        in_specs=in_specs,
        out_specs=out_specs,
        scratch_shapes=scratch,
        compiler_params=pltpu.CompilerParams(vmem_limit_bytes=vmem << 20),
        input_output_aliases=aliases,
        cost_estimate=pl.CostEstimate(flops=0, bytes_accessed=0, transcendentals=0),
    )(*arrays)


class Far:
    def __init__(self, value, space=pltpu.HBM):
        self.value, self.space = value, space


class Copies:
    def __init__(self, sems):
        self.sems, self.count, self.left = sems, 0, []

    def start(self, src, dst):
        copy = pltpu.make_async_copy(src, dst, self.sems.at[self.count])
        self.count += 1
        copy.start()
        self.left.append(copy)
        return copy

    def wait(self, *copies):
        for copy in copies:
            copy.wait()
            self.left.remove(copy)

    def finish(self):
        self.wait(*list(self.left))


def gate(value, deps):
    return pl.pallas_call(
        lambda *refs: None,
        out_shape=jax.ShapeDtypeStruct(value.shape, value.dtype),
        in_specs=[pl.BlockSpec(memory_space=pl.ANY)] * (1 + len(deps)),
        out_specs=pl.BlockSpec(memory_space=pl.ANY),
        input_output_aliases={0: 0},
        cost_estimate=pl.CostEstimate(flops=0, bytes_accessed=0, transcendentals=0),
    )(value, *deps)


def out(shape, dtype):
    return jax.ShapeDtypeStruct(shape, dtype)


def prep_kernel(rank_ref, side_ref, *refs):
    count = 18
    (x_hbm, win_hbm), refs = refs[:2], refs[2:]
    ins, outs, scratch = refs[:count], refs[count : count + 6], refs[count + 6 :]
    (core_hbm, near2_hbm, near3_hbm, *x_outs), scratch = scratch[:5], scratch[5:]
    held, (marks_ref, pack_ref, sems) = scratch[:count], scratch[count:]
    copies = Copies(sems)
    loads = [copies.start(src, dst) for src, dst in zip(ins, held)]
    for m, ref in enumerate(x_outs):
        copies.start(x_hbm.at[m, 0], ref)
    width = win_hbm.shape[1] // H
    size = win_hbm.shape[0] // 2
    for r, ref in ((1, core_hbm), (2, near2_hbm), (3, near3_hbm)):
        cols = pl.ds(pl.multiple_of((rank_ref[0] ^ r) * width, width), width)
        rows = pl.ds(pl.multiple_of((side_ref[0] % 2) * size, size), size) if r > 1 else slice(0, 2 * size)
        copies.start(win_hbm.at[rows, cols], ref)
    copies.wait(*loads)
    q_ref, k_ref, p_ref, rv_ref, ro_ref, v_ref, routes_v_ref, routes_o_ref = held[:8]
    seg_ref, pad_ref, g1_ref, b1_ref, g2_ref, b2_ref, bo_ref, cb_ref, pb_ref, bi_ref = held[8:]
    head_ref, bin_ref = outs[4:]
    head_ref[...] = jnp.zeros(head_ref.shape, f32)
    head_ref[0:1, 0:DH] = cb_ref[...].astype(f32).reshape(1, -1)
    head_ref[1:2, 0:DH] = pb_ref[...].astype(f32).reshape(1, -1)
    bin_ref[...] = bi_ref[...].astype(f32).reshape(1, -1)
    micro, own = seg_ref.shape[0], seg_ref.shape[2]
    marks_ref[...] = jnp.zeros(marks_ref.shape, f32)
    copied = [slice(0, own), slice(own, 2 * own)]
    for m in range(micro):
        for cols in copied:
            marks_ref[4 * m + 2 : 4 * m + 3, cols] = seg_ref[m].astype(f32)
            marks_ref[4 * m + 3 : 4 * m + 4, cols] = pad_ref[m].astype(f32)
    for i, ref in enumerate((g1_ref, b1_ref, g2_ref, b2_ref, bo_ref)):
        marks_ref[4 * micro + i : 4 * micro + i + 1, :] = ref[...].astype(f32).reshape(1, -1)
    row = lax.broadcasted_iota(jnp.int32, (16, H * E), 0)
    col = lax.broadcasted_iota(jnp.int32, (16, H * E), 1)
    for r in range(H):
        out_ref = outs[r] if r < 2 else pack_ref
        h = rank_ref[0] ^ r
        rows = pl.ds(pl.multiple_of(h * DH, 16), DH)
        for m in range(micro):
            for i, ref in enumerate((routes_v_ref, routes_o_ref)):
                ones = lax.shift_left(jnp.ones((2, own), jnp.int32), ref[m, h])
                code = jnp.sum(ones.astype(f32), axis=0, keepdims=True)
                for cols in copied:
                    marks_ref[4 * m + i : 4 * m + i + 1, cols] = code
        pick_v = jnp.where((row < E) & (col == h * E + row), 1.0, 0.0).astype(bf16)
        pick_o = jnp.where((row >= E) & (row < 2 * E) & (col == h * E + row - E), 1.0, 0.0)
        routers = mm(pick_v, rv_ref[...]) + mm(pick_o.astype(bf16), ro_ref[...])
        out_ref[0:DH, :] = q_ref[rows, :]
        out_ref[DH:LANE, :] = routers.astype(bf16)
        out_ref[LANE : LANE + DH, :] = k_ref[rows, :]
        out_ref[LANE + DH : 2 * LANE, :] = marks_ref[...].astype(bf16)
        out_ref[2 * LANE : 2 * LANE + DH, :] = p_ref[rows, :]
        out_ref[2 * LANE + DH : 3 * LANE, :] = jnp.zeros((LANE - DH, out_ref.shape[1]), bf16)
        for e in range(E):
            at = (3 + e) * LANE
            expert = pl.ds(pl.multiple_of((h * E + e) * DH, 16), DH)
            out_ref[at : at + DH, :] = v_ref[expert, :]
            out_ref[at + DH : at + LANE, :] = jnp.zeros((LANE - DH, out_ref.shape[1]), bf16)
        if r >= 2:
            half = pl.ds(pl.multiple_of((side_ref[0] % 2) * LANE, LANE), LANE)
            outs[r][...] = pack_ref[:, half]
    copies.finish()


def norm_stats(x):
    mean = jnp.mean(x, axis=-1, keepdims=True)
    centred = x - mean
    var = jnp.mean(centred * centred, axis=-1, keepdims=True)
    rstd = lax.rsqrt(var + 1e-05)
    return centred * rstd, rstd


def norm_back(grad, unit, rstd, gain):
    g = grad * gain
    return rstd * (
        g
        - jnp.mean(g, axis=-1, keepdims=True)
        - unit * jnp.mean(g * unit, axis=-1, keepdims=True)
    )


def x_send_keep(held, x_hbm, send_hbm, keep_hbm):
    return held[0], held[1], x_hbm, send_hbm, keep_hbm


def attention_kernel(m, rank_ref, side_ref, *refs):
    first = m == 0
    (x0, x1, x2, x3), refs = refs[:4], refs[4:]
    head_ref, refs = refs[0], refs[1:]
    if first:
        (w0, w1, near2, near3, far2, far3, sine_hbm, wo_hbm), refs = refs[:8], refs[8:]
    else:
        (wt_hbm, wo_hbm, pos_ref, vec_ref, rows_ref), refs = refs[:5], refs[5:]
    (x_ref, n_hbm, qc_hbm, qp_hbm, k_hbm, v_hbm, va_hbm, gate_hbm, p_hbm, att_hbm), refs = (
        refs[:10],
        refs[10:],
    )
    (mix_hbm, stat_ref), refs = refs[:2], refs[2:]
    (send_ref, keep_ref), refs = refs[:2], refs[2:]
    if first:
        (wt_hbm, wop_hbm, pos_ref, vec_ref, rows_ref), refs = refs[:5], refs[5:]
    n_ref, qc_ref, qp_ref, k_ref, v_ref, va_ref, gate_ref, p_ref, att_ref, mix_ref = refs[:10]
    wt_ref, wo_ref, x_out, send_out, keep_out = x_send_keep(refs[10:15], x_ref, send_ref, keep_ref)
    x_ref, send_ref, keep_ref = refs[12:15]
    sine_ref = refs[15] if first else None
    copies = Copies(refs[-1])
    length = x_ref.shape[0]
    both = slice(m * length, (m + 1) * length)
    blocks = length // BLK
    rank = rank_ref[0]
    quarter = D // H

    def at(r, size):
        return pl.ds(pl.multiple_of((rank ^ r) * size, size), size)

    loads = [copies.start(x0.at[m], x_ref.at[at(0, BLK), :])]
    loads += [copies.start(ref, x_ref.at[at(r, BLK), :]) for r, ref in enumerate((x1, x2, x3), 1)]
    if first:
        side = side_ref[0] % 2
        for r, ref in enumerate((w0, w1)):
            loads.append(copies.start(ref, wt_ref.at[:, at(r, quarter)]))
        for r, place, ref in (
            (2, side, near2),
            (3, side, near3),
            (2, 1 - side, far2),
            (3, 1 - side, far3),
        ):
            cols = pl.ds(pl.multiple_of((rank ^ r) * quarter + place * LANE, LANE), LANE)
            loads.append(copies.start(ref, wt_ref.at[:, cols]))
        sine_load = copies.start(sine_hbm, sine_ref)
        wo_loads = []
        for e in range(E):
            rows = slice(e * LANE, e * LANE + DH)
            wo_loads.append(copies.start(wo_hbm.at[e * DH : (e + 1) * DH, :], wo_ref.at[rows, :]))
            wo_ref[e * LANE + DH : (e + 1) * LANE, :] = jnp.zeros((LANE - DH, D), bf16)
        copies.wait(*loads)
        vec_ref[...] = jnp.zeros(vec_ref.shape, f32)
        rows_ref[...] = jnp.zeros(rows_ref.shape, f32)
        for r in range(H):
            micro = rows_ref.shape[0]
            marks = wt_ref[LANE + DH : 2 * LANE, at(r, quarter)].astype(f32)
            vec_ref[0:5, at(r, quarter)] = marks[4 * micro : 4 * micro + 5, :]
            fresh = pl.ds(pl.multiple_of((rank ^ r) * quarter + side * LANE, LANE), LANE)
            marks = wt_ref[LANE + DH : 2 * LANE, fresh].astype(f32)
            for i in range(micro):
                part = marks[4 * i : 4 * i + 4, :]
                rows_ref[i, 0:1, at(r, BLK)] = part[0:1, :] + 2.0**E * part[1:2, :]
                rows_ref[i, 1:3, at(r, BLK)] = part[2:4, :]
        copies.start(wt_ref, wt_hbm)
    else:
        wt_load = copies.start(wt_hbm, wt_ref)
        wo_loads = [copies.start(wo_hbm, wo_ref)]
        copies.wait(*loads)

    @pl.loop(0, blocks)
    def _(b):
        rows = pl.ds(pl.multiple_of(b * BLK, BLK), BLK)
        x = x_ref[rows, :].astype(f32)
        unit, rstd = norm_stats(x)
        n_ref[rows, :] = (unit * vec_ref[0:1, :] + vec_ref[1:2, :]).astype(bf16)
        first_lane = lax.broadcasted_iota(jnp.int32, (BLK, LANE), 1) == 0
        stat_ref[rows, :] = jnp.where(first_lane, jnp.mean(x, axis=-1, keepdims=True), rstd)

    copies.start(x_ref, x_out)
    copies.start(n_ref, n_hbm.at[both, :])
    if first:
        copies.wait(sine_load)
        pos_ref[...] = mm(sine_ref[...], wt_ref[2 * LANE : 3 * LANE, :], NT).astype(bf16)
    else:
        copies.wait(wt_load)
    lane = lax.broadcasted_iota(jnp.int32, (1, LANE), 1)
    is_head = lane < DH
    raw = mm(n_ref[...], wt_ref[0:LANE, :], NT)
    columns = rows_ref[m].T
    code = jnp.broadcast_to(columns[:, 0:1].astype(jnp.int32), (length, LANE))
    slot = jnp.where((lane >= DH) & (lane < DH + 2 * E), lane - DH, 31)
    pick = (lax.shift_right_logical(code, jnp.broadcast_to(slot, (length, LANE))) & 1) == 1
    gate = jnp.where(pick, 1.0 / (1.0 + jnp.exp(-raw)), 0.0)
    gate_ref[...] = gate
    copies.start(gate_ref, gate_hbm)
    qc_ref[...] = jnp.where(is_head, (raw + head_ref[0:1, :]) * SCALE, 0.0).astype(bf16)
    qp_ref[...] = jnp.where(is_head, (raw + head_ref[1:2, :]) * SCALE, 0.0).astype(bf16)
    keys = mm(n_ref[...], wt_ref[LANE : 2 * LANE, :], NT)
    k_ref[...] = jnp.where(is_head, keys, 0.0).astype(bf16)
    values = jnp.zeros((length, LANE), f32)
    for e in range(E):
        part = mm(n_ref[...], wt_ref[(3 + e) * LANE : (4 + e) * LANE, :], NT)
        va_ref[:, e * LANE : (e + 1) * LANE] = part.astype(bf16)
        values += part * gate[:, DH + e : DH + e + 1]
    v_ref[...] = values.astype(bf16)
    for src, dst in ((qc_ref, qc_hbm), (qp_ref, qp_hbm), (k_ref, k_hbm), (v_ref, v_hbm), (va_ref, va_hbm)):
        copies.start(src, dst)
    seg_col = columns[:, 1:2]
    for b in range(blocks):
        rows = slice(b * BLK, (b + 1) * BLK)
        wide = (b + 1) * BLK
        content = mm(qc_ref[rows, :], k_ref[0:wide, :], NT)
        table = mm(qp_ref[rows, :], pos_ref[length - wide : length, :], NT)
        table = pltpu.roll(table, (wide - BLK + 1) % wide, 1, stride=1, stride_axis=0)
        row = lax.broadcasted_iota(jnp.int32, (BLK, wide), 0) + b * BLK
        col = lax.broadcasted_iota(jnp.int32, (BLK, wide), 1)
        same = seg_col[rows, :] == rows_ref[m, 1:2, 0:wide]
        live = ((rows_ref[m, 2:3, 0:wide] > 0.0) & (col < row)) | (col == row)
        scores = jnp.where(same & live, content + table, MASKED)
        top = jnp.max(scores, axis=-1, keepdims=True)
        expo = jnp.exp(scores - top)
        prob = (expo / jnp.sum(expo, axis=-1, keepdims=True)).astype(bf16)
        p_ref[rows, 0:wide] = prob
        att = mm(prob, v_ref[0:wide, :])
        att_ref[rows, :] = att
        for e in range(E):
            share = gate_ref[rows, DH + E + e : DH + E + e + 1]
            mix_ref[rows, e * LANE : (e + 1) * LANE] = (att * share).astype(bf16)
        copies.start(p_ref.at[rows, 0:wide], p_hbm.at[rows, 0:wide])
    copies.start(att_ref, att_hbm)
    copies.start(mix_ref, mix_hbm.at[both, :])
    half = length // 2
    core = rank & 1
    copies.wait(*wo_loads)
    if first:
        copies.start(wo_ref, wop_hbm)
    for place, ref, dst in ((1 - core, send_ref, send_out), (core, keep_ref, keep_out)):
        rows = pl.ds(pl.multiple_of(place * half, half), half)
        ref[...] = mm(mix_ref[rows, :], wo_ref[...]).astype(bf16)
        copies.start(ref, dst)
    copies.finish()


def normal_terms(v):
    bell = jnp.exp(-0.5 * v * v)
    phi = 0.5 * (1.0 + lax.erf(v * (1.0 / math.sqrt(2.0))))
    return phi, bell * (1.0 / math.sqrt(2.0 * math.pi))


def pair_rows(core, b, refs):
    mine, far, mine2, far2 = refs
    own_half = (b // 2) == core
    rows = pl.ds(pl.multiple_of((b % 2) * BLK, BLK), BLK)
    near = mine[rows, :].astype(f32) + far[rows, :].astype(f32)
    away = mine2[rows, :].astype(f32) + far2[rows, :].astype(f32)
    return jnp.where(own_half, near, away)


def ffn_kernel(
    m,
    rank_ref,
    side_ref,
    x_hbm,
    a0,
    a1,
    a2,
    a3,
    vec_ref,
    bin_ref,
    win_hbm,
    win_core,
    *refs,
):
    (near2, near3, far2, far3), refs = refs[:4], refs[4:]
    (wout_hbm, c0, c1, c2, c3), refs = refs[:5], refs[5:]
    (n_hbm, hid_hbm, gp_hbm, cot_hbm, unit_hbm, rstd_ref, resid_ref, sum_ref), refs = (
        refs[:8],
        refs[8:],
    )
    (send_hbm, keep_hbm), refs = refs[:2], refs[2:]
    (unit_ref, win_ref, wout_ref, x_ref, n_ref, hid_ref, gp_ref, cot_ref), refs = refs[:8], refs[8:]
    halves, (send_ref, keep_ref, sems) = refs[:4], refs[4:]
    length = x_ref.shape[0]
    both = slice(m * length, (m + 1) * length)
    rank, place = rank_ref[0], side_ref[0]
    core = rank & 1
    copies = Copies(sems)
    size = D // H
    sum_ref[...] = jnp.zeros(sum_ref.shape, f32)

    def at(r, size):
        return pl.ds(pl.multiple_of((rank ^ r) * size, size), size)

    early = [copies.start(x_hbm, x_ref)]
    early += [copies.start(src, dst) for src, dst in zip((a0, a1, a2, a3), halves)]
    loads = []
    width = win_ref.shape[1]
    own_cols = pl.ds(pl.multiple_of(rank * width, width), width)
    loads.append(copies.start(win_hbm.at[:, own_cols], win_ref.at[at(0, size), :]))
    loads.append(copies.start(win_core, win_ref.at[at(1, size), :]))
    side = place % 2
    for r, half, ref in ((2, side, near2), (3, side, near3), (2, 1 - side, far2), (3, 1 - side, far3)):
        rows = pl.ds(pl.multiple_of((rank ^ r) * size + half * (size // 2), size // 2), size // 2)
        loads.append(copies.start(ref, win_ref.at[rows, :]))
    loads.append(copies.start(wout_hbm, wout_ref))
    for r, ref in enumerate((c0, c1, c2, c3)):
        loads.append(copies.start(ref.at[m], cot_ref.at[at(r, BLK), :]))

    copies.wait(*early)

    @pl.loop(0, length // BLK)
    def _(b):
        rows = pl.ds(pl.multiple_of(b * BLK, BLK), BLK)
        resid = x_ref[rows, :].astype(f32) + pair_rows(core, b, halves)
        unit, rstd = norm_stats(resid)
        unit_ref[rows, :] = unit.astype(bf16)
        rstd_ref[rows, :] = jnp.broadcast_to(rstd, (BLK, LANE))
        n_ref[rows, :] = (unit * vec_ref[2:3, :] + vec_ref[3:4, :]).astype(bf16)

        @pl.when(b == rank)
        def _():
            resid_ref[...] = resid

    copies.wait(*loads)
    for src, dst in (
        (unit_ref, unit_hbm),
        (n_ref, n_hbm.at[both, :]),
        (cot_ref, cot_hbm.at[both, :]),
    ):
        copies.start(src, dst)
    chunk = 256

    @pl.loop(0, width // chunk)
    def _(c):
        cols = pl.ds(pl.multiple_of(c * chunk, chunk), chunk)
        pre = mm(n_ref[...], win_ref[:, cols]) + bin_ref[0:1, cols]
        back = mm(cot_ref[...], wout_ref[cols, :], NT)
        phi, density = normal_terms(pre)
        hid_ref[:, cols] = (pre * phi).astype(bf16)
        grad = (back * (phi + pre * density)).astype(bf16)
        gp_ref[:, cols] = grad
        sum_ref[0:1, cols] = jnp.sum(grad.astype(f32), axis=0, keepdims=True)

    copies.start(hid_ref, hid_hbm.at[both, :])
    copies.start(gp_ref, gp_hbm.at[both, :])
    half = length // 2
    for place, ref, dst in ((1 - core, send_ref, send_hbm), (core, keep_ref, keep_hbm)):
        rows = pl.ds(pl.multiple_of(place * half, half), half)
        ref[...] = mm(gp_ref[rows, :], win_ref[...], NT).astype(bf16)
        copies.start(ref, dst)
    copies.finish()


def split_blocks(rank, value_ref, keep_ref, send_ref):
    for r in range(H):
        rows = pl.ds(pl.multiple_of((rank ^ r) * BLK, BLK), BLK)
        (send_ref if r % 2 else keep_ref)[r // 2] = value_ref[rows, :]


def project_kernel(rank_ref, side_ref, hid_hbm, wout_hbm, keep_hbm, send_hbm, *refs):
    hid_ref, wout_ref, full_ref, keep_ref, send_ref, sems = refs
    copies = Copies(sems)
    loads = [copies.start(wout_hbm, wout_ref), copies.start(hid_hbm, hid_ref)]
    copies.wait(*loads)
    full_ref[...] = mm(hid_ref[...], wout_ref[...]).astype(bf16)
    micro = keep_ref.shape[1]
    length = full_ref.shape[0] // micro
    for m in range(micro):
        for r in range(H):
            at = pl.multiple_of((rank_ref[0] ^ r) * BLK + m * length, BLK)
            ref = send_ref if r % 2 else keep_ref
            ref[r // 2, m] = full_ref[pl.ds(at, BLK), :]
    copies.start(keep_ref, keep_hbm)
    copies.start(send_ref, send_hbm)
    copies.finish()


def branch_kernel(m, rank_ref, side_ref, vec_ref, rstd_ref, gate_ref, att_ref, *refs):
    hbm, refs = refs[:7], refs[7:]
    (gb_hbm, sums_ref, grad_ref, ga_ref, logit_ref), refs = refs[:5], refs[5:]
    held, (gb_ref, sems) = refs[:7], refs[7:]
    copies = Copies(sems)
    *halves, cot_ref, unit_ref, wo_ref = held
    length = unit_ref.shape[0]
    both = slice(m * length, (m + 1) * length)
    hbm = [*hbm[:4], hbm[4].at[both, :], *hbm[5:]]
    *loads, wo_load = [copies.start(src, dst) for src, dst in zip(hbm, held)]
    rank = rank_ref[0]
    core = rank & 1
    sums_ref[...] = jnp.zeros(sums_ref.shape, f32)
    copies.wait(*loads)

    @pl.loop(0, length // BLK)
    def _(b):
        rows = pl.ds(pl.multiple_of(b * BLK, BLK), BLK)
        unit = unit_ref[rows, :].astype(f32)
        grad = pair_rows(core, b, halves)
        sums_ref[0:1, :] += jnp.sum(grad * unit, axis=0, keepdims=True)
        sums_ref[1:2, :] += jnp.sum(grad, axis=0, keepdims=True)
        cot = cot_ref[rows, :].astype(f32)
        sums_ref[2:3, :] += jnp.sum(cot, axis=0, keepdims=True)
        total = cot + norm_back(grad, unit, rstd_ref[rows, 0:1], vec_ref[2:3, :])
        gb_ref[rows, :] = total.astype(bf16)

        @pl.when(b == rank)
        def _():
            grad_ref[...] = total

    copies.start(gb_ref, gb_hbm.at[both, :])
    copies.wait(wo_load)
    lane = lax.broadcasted_iota(jnp.int32, (1, LANE), 1)
    acc = jnp.zeros((length, LANE), f32)
    logits = jnp.zeros((length, LANE), f32)
    for e in range(E):
        mixed = mm(gb_ref[...], wo_ref[e * LANE : (e + 1) * LANE, :], NT)
        acc += mixed * gate_ref[:, DH + E + e : DH + E + e + 1]
        dot = jnp.sum(mixed * att_ref[...], axis=-1, keepdims=True)
        logits = jnp.where(lane == DH + E + e, dot, logits)
    ga_ref[...] = acc.astype(bf16)
    logit_ref[...] = logits
    copies.finish()


def back_kernel(m, rank_ref, side_ref, ga_ref, logit_ref, pos_ref, gate_ref, stat_ref, *refs):
    hbm, refs = refs[:8], refs[8:]
    (sums_ref, dproj_hbm, gpos_ref, bias_ref, keep_hbm, send_hbm), refs = refs[:6], refs[6:]
    held, refs = refs[:8], refs[8:]
    dproj_ref, gk_ref, gv_ref, full_ref, keep_ref, send_ref, sems = refs
    copies = Copies(sems)
    *loads, va_load, wt_load, x_load = [copies.start(src, dst) for src, dst in zip(hbm, held)]
    p_ref, v_ref, k_ref, qc_ref, qp_ref, va_ref, wt_ref, x_ref = held
    length = x_ref.shape[0]
    blocks = length // BLK
    rank = rank_ref[0]
    lane = lax.broadcasted_iota(jnp.int32, (1, LANE), 1)
    sums_ref[...] = jnp.zeros(sums_ref.shape, f32)
    gk_ref[...] = jnp.zeros(gk_ref.shape, f32)
    gv_ref[...] = jnp.zeros(gv_ref.shape, f32)
    gpos_ref[...] = jnp.zeros(gpos_ref.shape, f32)
    row = lax.broadcasted_iota(jnp.int32, (BLK, BLK), 0)
    col = lax.broadcasted_iota(jnp.int32, (BLK, BLK), 1)
    mirror = jnp.where(row + col == BLK - 1, 1.0, 0.0).astype(bf16)
    cont_sum = jnp.zeros((1, LANE), f32)
    posn_sum = jnp.zeros((1, LANE), f32)
    copies.wait(*loads)
    for b in range(blocks):
        rows = slice(b * BLK, (b + 1) * BLK)
        wide = (b + 1) * BLK
        prob = p_ref[rows, 0:wide].astype(f32)
        ga = ga_ref[rows, :]
        grad_prob = mm(ga, v_ref[0:wide, :], NT)
        delta = jnp.sum(prob * grad_prob, axis=-1, keepdims=True)
        grad_score = (prob * (grad_prob - delta)).astype(bf16)
        gv_ref[0:wide, :] += mm(p_ref[rows, 0:wide], ga, TN)
        gk_ref[0:wide, :] += mm(grad_score, qc_ref[rows, :], TN)
        cont = mm(grad_score, k_ref[0:wide, :]) * SCALE
        table = pltpu.roll(mm(mirror, grad_score), 0, 1, stride=1, stride_axis=0)
        table = mm(mirror, table.astype(bf16)).astype(bf16)
        posn = mm(table, pos_ref[length - wide : length, :]) * SCALE
        gpos_ref[length - wide : length, :] += mm(table, qp_ref[rows, :], TN)
        cont_sum += jnp.sum(cont, axis=0, keepdims=True)
        posn_sum += jnp.sum(posn, axis=0, keepdims=True)
        dproj_ref[rows, 0:LANE] = (cont + posn).astype(bf16)
    bias_ref[...] = jnp.zeros(bias_ref.shape, f32)
    bias_ref[0:1, :] = cont_sum
    bias_ref[1:2, :] = posn_sum
    dproj_ref[:, LANE : 2 * LANE] = gk_ref[...].astype(bf16)
    dproj_ref[:, 2 * LANE : 3 * LANE] = jnp.zeros((length, LANE), bf16)
    copies.wait(va_load, wt_load, x_load)
    grad_values = gv_ref[...].astype(bf16).astype(f32)
    logits = logit_ref[...]
    for e in range(E):
        cols = slice((3 + e) * LANE, (4 + e) * LANE)
        dproj_ref[:, cols] = (grad_values * gate_ref[:, DH + e : DH + e + 1]).astype(bf16)
        dot = jnp.sum(grad_values * va_ref[:, e * LANE : (e + 1) * LANE].astype(f32), axis=-1, keepdims=True)
        logits = jnp.where(lane == DH + e, dot, logits)
    gate = gate_ref[...]
    logits = logits * gate * (1.0 - gate)
    dproj_ref[:, 0:LANE] = jnp.where(
        lane < DH, dproj_ref[:, 0:LANE].astype(f32), logits
    ).astype(bf16)
    copies.start(dproj_ref, dproj_hbm.at[m * length : (m + 1) * length, :])
    chunk = 256
    mean, rstd = stat_ref[:, 0:1], stat_ref[:, 1:2]

    @pl.loop(0, D // chunk)
    def _(c):
        cols = pl.ds(pl.multiple_of(c * chunk, chunk), chunk)
        part = mm(dproj_ref[...], wt_ref[:, cols])
        full_ref[:, cols] = part.astype(bf16)
        unit = (x_ref[:, cols].astype(f32) - mean) * rstd
        sums_ref[3:4, cols] = jnp.sum(part * unit, axis=0, keepdims=True)
        sums_ref[4:5, cols] = jnp.sum(part, axis=0, keepdims=True)

    split_blocks(rank, full_ref, keep_ref, send_ref)
    copies.start(send_ref, send_hbm)
    copies.start(keep_ref, keep_hbm)
    copies.finish()


def output_kernel(rank_ref, side_ref, vec_ref, keep_ref, got_ref, far_ref, *refs):
    y_ref = refs[-1]
    for m in range(y_ref.shape[0]):
        total = refs[m][...] + keep_ref[0, m].astype(f32) + got_ref[0, m].astype(f32)
        y_ref[m, 0] = (total + far_ref[m].astype(f32) + vec_ref[4:5, :]).astype(bf16)


def input_kernel(rank_ref, side_ref, x_ref, vec_ref, far_ref, *refs):
    y_ref = refs[-1]
    for m in range(y_ref.shape[0]):
        grad_ref, keep_ref, got_ref = refs[3 * m : 3 * m + 3]
        unit, rstd = norm_stats(x_ref[m].astype(f32))
        back = keep_ref[0].astype(f32) + got_ref[0].astype(f32) + far_ref[m].astype(f32)
        y_ref[m, 0] = grad_ref[...] + norm_back(back, unit, rstd, vec_ref[0:1, :])


def vectors_kernel(
    rank_ref, side_ref, sums0, sums1, norm0, norm1, bias0, bias1, hid0, hid1, y_ref
):
    y_ref[...] = jnp.zeros(y_ref.shape, f32)
    width = D // H
    own = pl.ds(pl.multiple_of(rank_ref[0] * width, width), width)
    y_ref[0, 6:7, :] = norm0[3:4, :] + norm1[3:4, :]
    y_ref[1, 6:7, :] = norm0[4:5, :] + norm1[4:5, :]
    for i in range(3):
        y_ref[i, 7:8, own] = sums0[i : i + 1, own] + sums1[i : i + 1, own]
    for i in range(2):
        cols = pl.ds(pl.multiple_of(rank_ref[0] * width + i * LANE, LANE), LANE)
        y_ref[3, 7:8, cols] = bias0[i : i + 1, :] + bias1[i : i + 1, :]
    for i in range(4):
        cols = slice(i * width, (i + 1) * width)
        y_ref[4 + i, 7:8, own] = hid0[0:1, cols] + hid1[0:1, cols]


def load_ffn_chunk(copies, c, sources, dst):
    grad_o, grad_i = sources
    rows = D // RING
    part = rows // H
    copies.start(grad_o.at[pl.ds(pl.multiple_of(c * rows, rows), rows), :], dst.at[0:rows, :])
    for s in range(H):
        src = pl.ds(pl.multiple_of(s * (D // H) + c * part, part), part)
        copies.start(grad_i.at[src, :], dst.at[rows + s * part : rows + (s + 1) * part, :])


def load_pack_chunk(copies, c, sources, dst):
    grad_p, grad_w = sources
    rows = D // RING
    part = E * LANE // RING
    copies.start(grad_p.at[pl.ds(pl.multiple_of(c * rows, rows), rows), :], dst.at[0:rows, :])
    copies.start(
        grad_w.at[pl.ds(pl.multiple_of(c * part, part), part), :], dst.at[rows : rows + part, :]
    )


def ring_kernel(load, split, t, rank_ref, pos_ref, src0, src1, *refs):
    tail_ref, refs = (refs[0], refs[1:]) if load is load_pack_chunk else (None, refs)
    got_hbm, refs = (refs[:2], refs[2:]) if t else ((), refs)
    outs_hbm, refs = (refs[:2], refs[2:]) if t < 4 else (refs[: 1 + H], refs[1 + H :])
    loaded, held, *more, sems = refs
    got, outs = more[: len(got_hbm)], more[len(got_hbm) :]
    copies = Copies(sems)
    for src, dst in zip(got_hbm, got):
        copies.start(src, dst)
    pos = pos_ref[0]
    total = held.shape[1]
    chunks = [(pos + 4 - t) % RING, (pos + 4 + t) % RING][: 2 if t < 4 else 1]
    for i, c in enumerate(chunks[: 2 if t < 4 else 1]):
        load(copies, c, (src0, src1), loaded.at[i])
    copies.finish()
    held[...] = loaded[...].astype(f32)
    if tail_ref is not None:
        for i, c in enumerate(chunks):
            rows = slice(D // RING - TAIL, D // RING)
            held[i, rows, :] = held[i, rows, :] + tail_ref[c]
    if t == 4:
        held[0] = held[0] + got[0][...].astype(f32) + got[1][...].astype(f32)
        rows = D // RING
        rank = rank_ref[0]
        for r, ref in enumerate(outs[1:]):
            if tail_ref is None:
                size = rows // H
                at = pl.multiple_of(rows + (rank ^ r) * size, size)
                ref[...] = held[0, pl.ds(at, size), :].astype(bf16)
            else:
                size = D // H
                at = pl.multiple_of((rank ^ r) * size, size)
                ref[...] = held[0, 0:rows, pl.ds(at, size)].astype(bf16)
        outs[0][...] = (held[0, 0:rows, :] if tail_ref is None else held[0, rows:total, :]).astype(bf16)
        for ref, dst in zip(outs, outs_hbm):
            copies.start(ref, dst)
        copies.finish()
        return
    for i, ref in enumerate(outs):
        part = slice(0, split) if i == 0 else slice(split, total)
        if t == 0:
            ref[...] = held[i, part, :].astype(bf16)
        elif t == 1:
            ref[...] = held[i].astype(bf16)
            ref[part, :] = (held[i, part, :] + got[i][...].astype(f32)).astype(bf16)
        else:
            ref[...] = (held[i] + got[i][...].astype(f32)).astype(bf16)
        copies.start(ref, outs_hbm[i])
    copies.finish()


def load_ring(copies, pos, split, refs, dst):
    own, fwd, bwd, half_fwd, half_bwd = refs[0], refs[1:4], refs[4:7], refs[7], refs[8]
    copies.start(own, dst.at[pos])
    for i in range(3):
        copies.start(fwd[i], dst.at[(pos + RING - 1 - i) % RING])
        copies.start(bwd[i], dst.at[(pos + 1 + i) % RING])
    last = (pos + 4) % RING
    copies.start(half_fwd, dst.at[last, 0:split, :])
    copies.start(half_bwd, dst.at[last, split : dst.shape[1], :])
    copies.finish()


def ffn_grads_kernel(split, rank_ref, pos_ref, *refs):
    parts, (o_hbm, i_hbm, held, o_ref, i_ref, sems) = refs[:9], refs[9:]
    copies = Copies(sems)
    load_ring(copies, pos_ref[0], split, parts, held)
    rows = D // RING
    part = rows // H
    for c in range(RING):
        o_rows = slice(c * rows, (c + 1) * rows)
        o_ref[o_rows, :] = held[c, 0:rows, :].astype(f32)
        copies.start(o_ref.at[o_rows, :], o_hbm.at[o_rows, :])
        i_rows = slice(c * part, (c + 1) * part)
        for r in range(H):
            cols = pl.ds(pl.multiple_of((rank_ref[0] ^ r) * D, D), D)
            at = rows + r * part
            i_ref[i_rows, cols] = held[c, at : at + part, :].astype(f32)
        copies.start(i_ref.at[i_rows, :], i_hbm.at[i_rows, :])
    copies.finish()


def pack_grads_kernel(split, rank_ref, pos_ref, *refs):
    parts, refs = refs[:9], refs[9:]
    (q_ref, rv_ref, ro_ref, k_ref, p_ref, v_ref, w_ref), refs = refs[:7], refs[7:]
    (g1, b1, g2, b2, bo, content, posn, bin_ref), refs = refs[:8], refs[8:]
    held, heads, sems = refs
    copies = Copies(sems)
    load_ring(copies, pos_ref[0], split, parts, held)
    width = D // H
    rank = rank_ref[0]
    for r in range(H):
        heads[rank ^ r] = held[:, 0:LANE, r * width : (r + 1) * width].astype(f32)
    for h in range(H):
        rows = slice(h * DH, (h + 1) * DH)
        q_ref[rows, :] = heads[h, 0, 0:DH, :]
        rv_ref[h * E : (h + 1) * E, :] = heads[h, 0, DH : DH + E, :]
        ro_ref[h * E : (h + 1) * E, :] = heads[h, 0, DH + E : DH + 2 * E, :]
        k_ref[rows, :] = heads[h, 1, 0:DH, :]
        p_ref[rows, :] = heads[h, 2, 0:DH, :]
        for e in range(E):
            at = (h * E + e) * DH
            v_ref[at : at + DH, :] = heads[h, 3 + e, 0:DH, :]
    part = E * LANE // RING
    for c in range(RING):
        for e in range(E):
            low, high = max(c * part, e * LANE), min((c + 1) * part, e * LANE + DH)
            if low < high:
                at = low - e * LANE + e * DH
                w_ref[at : at + high - low, :] = held[
                    c, LANE + low - c * part : LANE + high - c * part, :
                ].astype(f32)
    last = slice(LANE - 1, LANE)
    before = slice(LANE - 2, LANE - 1)
    for ref, c in ((g1, 0), (b1, 1)):
        ref[...] = sum(heads[h, c, before, :] for h in range(H)).reshape(ref.shape)
    for c, ref in enumerate((g2, b2, bo)):
        ref[...] = heads[rank, c, last, :].reshape(ref.shape)
    row = heads[rank, 3, last, :]
    content[...] = row[:, 0:DH].reshape(content.shape)
    posn[...] = row[:, LANE : LANE + DH].reshape(posn.shape)
    for i in range(4):
        bin_ref[i * width : (i + 1) * width] = heads[rank, 4 + i, last, :].reshape((width,))


def flip_shard(value, bit):
    return lax.ppermute(value, "shard", [(s, s ^ bit) for s in range(H)])


def flip_dp(value, bit):
    count = lax.axis_size("dp")
    return lax.ppermute(value, "dp", [(d, d ^ bit) for d in range(count)])


def take(value, at, size, axis=0):
    return lax.dynamic_slice_in_dim(value, at, size, axis)


def put(value, part, at, axis=0):
    return lax.dynamic_update_slice_in_dim(value, part, at, axis)


def spread(own):
    across = flip_shard(own, 2)
    return own, flip_shard(own, 1), across, flip_shard(across, 1)


def ring_order():
    return list(range(0, RING, 2)) + list(range(RING - 1, 0, -2))


def pass_on(value, way):
    order, count = ring_order(), lax.axis_size("dp")
    pairs = [
        (base + order[i], base + order[(i + way) % RING])
        for base in range(0, count, RING)
        for i in range(RING)
    ]
    return lax.ppermute(value, "dp", pairs)


def swap_shard(value, rank, size, axis):
    parts = [take(value, (rank ^ r) * size, size, axis) for r in range(H)]
    return [flip_shard(p, r) if r else p for r, p in enumerate(parts)]


def sinusoid(length, feature_count):
    distance = (length - 1 - jnp.arange(length, dtype=jnp.int32)).astype(f32)
    inv_freq = jnp.exp(
        jnp.arange(0, feature_count, 2, dtype=jnp.int32).astype(f32)
        * (-math.log(10000.0) / feature_count)
    )
    angles = distance[:, None] * inv_freq[None, :]
    return jnp.concatenate([jnp.sin(angles), jnp.cos(angles)], axis=1)


def local(
    inputs,
    segments,
    padding,
    routes_value,
    routes_output,
    norm1_gain,
    norm1_bias,
    query_weight,
    key_weight,
    pos_weight,
    content_bias,
    pos_bias,
    value_router,
    output_router,
    value_experts,
    output_experts,
    norm2_gain,
    norm2_bias,
    ffn_in,
    ffn_in_bias,
    ffn_out,
    ffn_out_bias,
    cotangent,
):
    micro = inputs.shape[0]
    own = inputs.shape[2]
    length = own * H
    dp_count = lax.axis_size("dp")
    rank = lax.axis_index("shard")
    me = rank.astype(jnp.int32).reshape(1)
    dp_rank = lax.axis_index("dp")
    side = (dp_rank % RING).astype(jnp.int32).reshape(1)
    place = dp_rank % RING
    place = jnp.where(place % 2 == 0, place // 2, RING - 1 - place // 2)
    place = place.astype(jnp.int32).reshape(1)
    quarter = D // H

    token = [me]

    def after(value, *deps):
        return lax.optimization_barrier((value, *deps))[0]

    def step(fn, first, *rest):
        res = fn(after(first, token[0]), *rest)
        token[0] = jax.tree.leaves(res)[0]
        return res

    def kernel(fn, outs, args, second=side, **kwargs):
        deps = [*kwargs.pop("deps", ()), *([] if token[0] is me else [token[0]])]
        res = call(fn, outs, [me, second, *args], deps=deps, **kwargs)
        token[0] = res[0]
        return res

    packs = kernel(
        prep_kernel,
        [out((PACK, quarter), bf16)] * 2
        + [out((PACK, LANE), bf16)] * 2
        + [out((8, LANE), f32), out((1, FF // H), f32)]
        + [out((quarter, FF // H), bf16)]
        + [out((quarter // 2, FF // H), bf16)] * 2
        + [out((own, D), bf16)] * micro,
        [
            Far(a)
            for a in (
                inputs,
                ffn_in,
                query_weight.T,
                key_weight.T,
                pos_weight.T,
                value_router.T,
                output_router.T,
                value_experts.T,
                routes_value[:, 0].transpose(0, 2, 3, 1),
                routes_output[:, 0].transpose(0, 2, 3, 1),
                segments,
                padding,
                norm1_gain,
                norm1_bias,
                norm2_gain,
                norm2_bias,
                ffn_out_bias,
                content_bias,
                pos_bias,
                ffn_in_bias,
            )
        ],
        scratch=[
            pltpu.VMEM(shape, dtype)
            for shape, dtype in [((H * DH, quarter), bf16)] * 3
            + [((H * E, quarter), bf16)] * 2
            + [((H * E * DH, quarter), bf16)]
            + [((micro, H, 2, own), jnp.int32)] * 2
            + [((micro, 1, own), jnp.int32)] * 2
            + [((quarter,), bf16)] * 5
            + [((DH,), bf16)] * 2
            + [((FF // H,), bf16)]
            + [((LANE - DH, quarter), f32), ((PACK, quarter), bf16)]
        ],
        copies=18 + 3 + micro,
        vmem=56,
    )
    sine = sinusoid(length, D).astype(bf16)
    head, b_in, core_in, *sent = packs[H:]
    sent_in, sent_x = sent[:2], sent[2:]
    near = [flip_shard(packs[r], r) for r in (2, 3)]
    w_core = flip_shard(packs[1], 1)
    far = [flip_dp(w, 1) for w in near]
    weights = [packs[0], w_core, *near, *far]
    x_own = inputs[:, 0]
    sent_x[0] = gate(sent_x[0], [*near, sine])
    x_parts = [spread(x) for x in sent_x]
    near_in = [flip_shard(w, r) for w, r in zip(sent_in, (2, 3))]
    w_in_core = flip_shard(core_in, 1)
    cot_parts = spread(cotangent[:, 0])

    def add_chip(keep, send):
        got = flip_shard(send, 1)
        add = lambda k, g: (k.astype(f32) + g.astype(f32)).astype(bf16)
        return step(add, keep, got)

    def finish_halves(chip):
        across = flip_shard(chip, 2)
        return chip, across, flip_shard(chip, 1), flip_shard(across, 1)

    half = out((length // 2, D), bf16)
    wide = out((length, D), bf16)
    saved_shapes = (
        [wide]
        + [out((length, LANE), bf16)] * 4
        + [
            out((length, E * LANE), bf16),
            out((length, LANE), f32),
            out((length, length), bf16),
            out((length, LANE), f32),
            out((length, E * LANE), bf16),
        ]
    )
    vmem_of = lambda shapes: [pltpu.VMEM(o.shape, o.dtype) for o in shapes]
    weight_shapes = [out((PACK, D), bf16), out((E * LANE, D), bf16)]
    joined = out((micro * length, D), bf16)
    saved = []
    residuals = []
    for m in range(micro):
        if m == 0:
            more = [Far(w) for w in weights] + [Far(sine), Far(output_experts)]
            extra = [Far(o) for o in weight_shapes]
            extra += [out((length, LANE), bf16), out((8, D), f32), out((micro, 8, length), f32)]
        else:
            more = [Far(wt), Far(w_out_heads), pos, vec, rows]
            extra = []
        res = kernel(
            functools.partial(attention_kernel, m),
            [Far(wide)]
            + [Far(joined)]
            + [Far(o) for o in saved_shapes[1:-1]]
            + [Far(out((micro * length, E * LANE), bf16))]
            + [out((length, LANE), f32), Far(half), Far(half)]
            + extra,
            [Far(x) for x in (x_own, *x_parts[m][1:])] + [head] + more,
            scratch=vmem_of(
                saved_shapes + weight_shapes + [wide, half, half] + ([wide] if m == 0 else [])
            ),
            copies=40,
            into={1: saved[0][1], 10: saved[0][10]} if m else None,
            deps=[*near_in, residuals[0][0]] if m else [],
            vmem=60,
            flops=2 * length * D * 1700,
        )
        saved.append(res[:12])
        if m == 0:
            near_in = [gate(w, [res[12]]) for w in near_in]
            far_in = [flip_dp(w, 1) for w in near_in]
        send, keep = res[12:14]
        if m == 0:
            wt, w_out_heads, pos, vec, rows = res[14:]
            send = gate(send, [*near_in, *x_parts[1][1:3]][: 4])
        else:
            send = gate(send, [*far_in, cot_parts[2], residuals[0][1]])
        residuals.append(finish_halves(add_chip(keep, send)))
    ffn = []
    gn2 = []
    for m in range(micro):
        res = kernel(
            functools.partial(ffn_kernel, m),
            [Far(joined)] * 4
            + [Far(wide)]
            + [
                out((length, LANE), f32),
                out((own, D), f32),
                out((8, FF // H), f32),
                Far(half),
                Far(half),
            ],
            [Far(a) for a in (saved[m][0], *residuals[m])]
            + [vec, b_in]
            + [Far(w) for w in (ffn_in, w_in_core, *near_in, *far_in, ffn_out, *cot_parts)],
            scratch=vmem_of(
                [wide, out((D, FF // H), bf16), out((FF // H, D), bf16)] + [wide] * 5 + [half] * 6
            ),
            copies=30,
            into={i: ffn[0][i] for i in range(4)} if m else None,
            vmem=60,
            deps=[residuals[1][0] if m == 0 else gn2[0][0]],
            flops=2 * length * D * D * 3,
        )
        ffn.append(res)
        gn2.append(finish_halves(add_chip(res[-1], res[-2])))

    def tn(a, b):
        return mm(a, b, TN).astype(bf16)

    class Ring:
        def __init__(self, load, split, total, sources):
            self.load, self.split, self.total = load, split, total
            self.sources, self.got, self.t = sources, (), 0

        def step(self, deps=()):
            rows = D // RING
            if self.t == 0:
                shapes = [(self.split, D), (self.total - self.split, D)]
            elif self.t < 4:
                shapes = [(self.total, D)] * 2
            elif len(self.sources) == 2:
                shapes = [(rows, D)] + [(rows // H, D)] * H
            else:
                shapes = [(self.total - rows, D)] + [(rows, D // H)] * H
            shapes = [out(shape, bf16) for shape in shapes]
            res = kernel(
                functools.partial(ring_kernel, self.load, self.split, self.t),
                [Far(o) for o in shapes],
                [Far(g) for g in self.sources[:2]]
                + list(self.sources[2:])
                + [Far(g) for g in self.got],
                second=place,
                scratch=[pltpu.VMEM((2, self.total, D), bf16), pltpu.VMEM((2, self.total, D), f32)]
                + vmem_of(self.got)
                + vmem_of(shapes),
                copies=20,
                deps=deps,
                vmem=56,
            )
            self.t += 1
            self.sent = res[0]
            if self.t == 5:
                return [self.across(p) for p in res]
            self.got = (pass_on(res[0], 1), pass_on(res[1], -1))

        def across(self, piece):
            bit = RING
            while bit < dp_count:
                piece = (piece.astype(f32) + flip_dp(piece, bit).astype(f32)).astype(bf16)
                bit *= 2
            return piece

        def gather(self, piece):
            self.parts = [[piece], [piece]]
            self.pass_parts()

        def pass_parts(self):
            for way, parts in zip((1, -1), self.parts):
                value = parts[-1]
                if len(parts) == 4:
                    cut = (lambda v: v[: self.split]) if way == 1 else (lambda v: v[self.split :])
                    value = step(cut, value)
                parts.append(pass_on(value, way))

        def result(self):
            fwd, bwd = self.parts
            return [fwd[0], *fwd[1:4], *bwd[1:4], fwd[4], bwd[4]]

    n2, hid, gp, cots = ffn[1][:4]
    grad_o = tn(hid, cots)
    grad_i = tn(n2, gp)
    ffn_ring = Ring(load_ffn_chunk, D // RING, 2 * D // RING, [grad_o, grad_i])
    ffn_ring.step()
    back = []

    branch = []

    def run_branch(m, deps=()):
        gate_m, att, rstd = saved[m][7], saved[m][9], ffn[m][5]
        from_far = [*gn2[m], ffn[1][3], ffn[m][4], w_out_heads]
        branch.append(
            kernel(
                functools.partial(branch_kernel, m),
                [
                    Far(joined),
                    out((8, D), f32),
                    out((own, D), f32),
                    out((length, LANE), bf16),
                    out((length, LANE), f32),
                ],
                [vec, rstd, gate_m, att] + [Far(a) for a in from_far],
                copies=10,
                vmem=56,
                deps=deps,
                scratch=vmem_of([*from_far[:4], wide, *from_far[5:], wide]),
                into={0: branch[0][0]} if m else None,
            )
        )

    def run_back(m, deps=()):
        x, n1, qc, qp, k, v, va, gate_m, prob, att, mix, stat = saved[m]
        from_far = [prob, v, k, qc, qp, va, wt, x]
        back.append(
            kernel(
                functools.partial(back_kernel, m),
                [
                    out((8, D), f32),
                    Far(out((micro * length, PACK), bf16)),
                    out((length, LANE), f32),
                    out((8, LANE), f32),
                    Far(out((2, own, D), bf16)),
                    Far(out((2, own, D), bf16)),
                ],
                [branch[m][3], branch[m][4], pos, gate_m, stat] + [Far(a) for a in from_far],
                copies=12,
                into={1: back[0][1]} if m else None,
                vmem=56,
                deps=deps,
                scratch=vmem_of(from_far)
                + [
                    pltpu.VMEM((length, PACK), bf16),
                    pltpu.VMEM((length, LANE), f32),
                    pltpu.VMEM((length, LANE), f32),
                    pltpu.VMEM((length, D), bf16),
                    pltpu.VMEM((2, own, D), bf16),
                    pltpu.VMEM((2, own, D), bf16),
                ],
            )
        )

    run_branch(0)
    ffn_ring.step()
    run_back(0)
    ffn_ring.step()
    run_branch(1)
    ffn_ring.step()
    grad_w = tn(saved[1][10], branch[1][0])
    run_back(1, deps=[grad_w])
    turned = lambda parts: [flip_shard(p, r) if r else p for r, p in enumerate(parts)]
    piece, *parts = ffn_ring.step()
    ffn_piece = jnp.concatenate([piece, *turned(parts)])
    gpos = (back[0][2] + back[1][2]).astype(bf16)
    grad_p = tn(gate(back[1][1], [piece]), saved[1][1])
    grad_p = lax.dynamic_update_slice(grad_p, tn(gpos, sine), (2 * LANE, 0))
    tails = kernel(
        vectors_kernel,
        [out((RING, TAIL, D), f32)],
        [branch[0][1], branch[1][1], back[0][0], back[1][0], back[0][3], back[1][3]]
        + [ffn[0][7], ffn[1][7]],
    )[0]
    pack_ring = Ring(
        load_pack_chunk, DH, D // RING + E * LANE // RING, [grad_p, grad_w, tails]
    )
    ffn_ring.gather(ffn_piece)
    pack_ring.step()
    add = lambda a, b: (a.astype(f32) + b.astype(f32)).astype(bf16)
    gx_got = [flip_shard(back[m][5], 1) for m in range(micro)]
    gx_far = jnp.stack([add(back[m][4][1], gx_got[m][1]) for m in range(micro)])
    gx_far = flip_shard(gx_far, 2)
    came = lambda i: [p[i] for p in ffn_ring.parts]
    both_ways = ffn_ring.parts
    both_ways[0][1] = gate(both_ways[0][1], [pack_ring.sent, both_ways[1][1]])
    for i in range(1, 4):
        ffn_ring.pass_parts()
        pack_ring.step(deps=came(i + 1))
    gx_all = kernel(
        input_kernel,
        [out((micro, 1, own, D), f32)],
        [x_own, vec, gx_far]
        + [a for m in range(micro) for a in (branch[m][2], back[m][4], gx_got[m])],
    )[0]
    piece, *parts = pack_ring.step()
    pack_piece = jnp.concatenate([jnp.concatenate(turned(parts), axis=1), piece])
    pack_ring.gather(pack_piece)
    g_out, g_in = kernel(
        functools.partial(ffn_grads_kernel, ffn_ring.split),
        [Far(out((FF // H, D), f32)), Far(out((quarter, FF), f32))],
        [Far(p) for p in ffn_ring.result()],
        second=place,
        scratch=[
            pltpu.VMEM((RING, ffn_ring.total, D), bf16),
            pltpu.VMEM((FF // H, D), f32),
            pltpu.VMEM((quarter, FF), f32),
        ],
        copies=25,
        vmem=40,
        deps=[pack_piece],
    )
    ways = pack_ring.parts
    sides = out((2, micro, own, D), bf16)
    keep, send = kernel(
        project_kernel,
        [Far(sides)] * 2,
        [Far(hid), Far(ffn_out)],
        scratch=vmem_of([joined, out((FF // H, D), bf16), joined, sides, sides]),
        copies=4,
        vmem=56,
        deps=[pack_piece],
    )
    ways[0][1] = gate(ways[0][1], [g_out, keep, ways[1][1]])
    got = flip_shard(gate(send, [ways[0][1]]), 1)
    far = flip_shard(add(keep[1], got[1]), 2)
    pack_ring.pass_parts()
    pack_ring.pass_parts()
    pack_ring.pass_parts()
    y_all = kernel(
        output_kernel,
        [out((micro, 1, own, D), bf16)],
        [vec, keep, got, far] + [ffn[m][6] for m in range(micro)],
    )[0]
    res = kernel(
        functools.partial(pack_grads_kernel, pack_ring.split),
        [
            out((H * DH, quarter), f32),
            out((H * E, quarter), f32),
            out((H * E, quarter), f32),
            out((H * DH, quarter), f32),
            out((H * DH, quarter), f32),
            out((H * E * DH, quarter), f32),
            out((E * DH, D), f32),
        ]
        + [out((quarter,), f32)] * 5
        + [out((DH,), f32)] * 2
        + [out((FF // H,), f32)],
        [Far(p) for p in pack_ring.result()],
        second=place,
        scratch=[
            pltpu.VMEM((RING, pack_ring.total, D), bf16),
            pltpu.VMEM((H, RING, LANE, quarter), f32),
        ],
        copies=9,
        vmem=40,
    )
    g_q, g_rv, g_ro, g_k, g_p, g_v, g_wo, g1, b1, g2, b2, bo, content, posb, bi = res
    return (
        y_all,
        gx_all,
        g1,
        b1,
        g_q.T,
        g_k.T,
        g_p.T,
        content,
        posb,
        g_rv.T,
        g_ro.T,
        g_v.T,
        g_wo,
        g2,
        b2,
        g_in,
        bi,
        g_out,
        bo,
    )


def solution(mesh):
    tokens = P(None, "dp", "shard")
    whole = P(None, "dp", "shard", None)
    routes = P(None, "dp", "shard", None, None)
    vector = P("shard")
    matrix = P("shard", None)
    weights = (
        vector,
        vector,
        matrix,
        matrix,
        matrix,
        vector,
        vector,
        matrix,
        matrix,
        matrix,
        matrix,
        vector,
        vector,
        matrix,
        vector,
        matrix,
        vector,
    )
    return jax.shard_map(
        local,
        mesh=mesh,
        in_specs=(whole, tokens, tokens, routes, routes) + weights + (whole,),
        out_specs=(whole, whole) + weights,
        check_vma=False,
    )
```

profile of v0, /device:TPU:0, one launch (start us, length us, event | category | flops | bytes accessed | tf_op | source)
XLA Modules:
  0.0 357.5 jit_solution(7789790227300135016)
XLA Ops:
  0.7 4.1 %shard_map.366 = (bf16[1024,256]{1,0:T(8,128)(2,1)}, bf16[1024,256]{1,0:T(8,128)(2,1)}, bf16[1024,128]{1,0:T(8,128)(2,1)}, bf16[1024,128]{1,0:T(8,128)(2,1)}, f3...) custom-call(s32[1]{0:T(128)} %bitcast.rank_ref.refs_0_, ...), custom_call_target="tpu_custom_call" | custom-call | tf_op jit(solution)/shard_map/pallas_call | solution.py:57
  4.8 3.0 collective-permute-start
  8.0 4.1 %fusion.1 = (bf16[512,512]{1,0:T(8,128)(2,1)S(1)}, bf16[512,512]{1,0:T(8,128)(2,1)S(1)}) fusion(f32[512]{0:T(512)S(1)} %multiply_exponential_fusion, f32[512]{0:T(512)S(1)} %subtract_convert_fusion), kind=kLoop, calls=%fused_computation.8 | loop fusion | flops 786432 | bytes 1052672 | tf_op jit(solution)/shard_map/convert
  15.1 4.2 %collective-permute-done.1.refs_2_.refs_10_ = bf16[1024,128]{1,0:T(8,128)(2,1)S(1)} collective-permute-done((bf16[1024,128]{1,0:T(8,128)(2,1)}, bf16[1024,128]{1,0:T(8,128)(2,1)S(1)}, u32[]{:S(2)}, u32[]{:S(2)}) %collective-permute-start.1) | collective-permute-done | bytes 262176 | tf_op jit(solution)/shard_map/ppermute | solution.py:775
  23.9 4.9 %collective-permute-done.3.refs_4_ = bf16[128,1024]{1,0:T(8,128)(2,1)S(1)} collective-permute-done((bf16[128,1024]{1,0:T(8,128)(2,1)}, bf16[128,1024]{1,0:T(8,128)(2,1)S(1)}, u32[]{:S(2)}, u32[]{:S(2)}) %collective-permute-start.3) | collective-permute-done | bytes 262176 | tf_op jit(solution)/shard_map/ppermute | solution.py:775
  28.9 1.9 collective-permute-start.12
  31.5 4.4 %collective-permute-done.7.refs_12_ = bf16[1024,128]{1,0:T(8,128)(2,1)S(1)} collective-permute-done((bf16[1024,128]{1,0:T(8,128)(2,1)}, bf16[1024,128]{1,0:T(8,128)(2,1)S(1)}, u32[]{:S(2)}, u32[]{:S(2)}) %collective-permute-start.7) | collective-permute-done | bytes 262176 | tf_op jit(solution)/shard_map/ppermute | solution.py:780
  37.4 10.7 %shard_map.368 = (bf16[512,1024]{1,0:T(8,128)(2,1)}, bf16[1024,1024]{1,0:T(8,128)(2,1)}, bf16[512,128]{1,0:T(8,128)(2,1)}, bf16[512,128]{1,0:T(8,128)(2,1)}, bf1...) custom-call(s32[1]{0:T(128)} %bitcast.rank_ref.refs_0_, ...), custom_call_target="tpu_custom_call" | custom-call | tf_op jit(solution)/shard_map/pallas_call | solution.py:57
  58.4 10.5 %shard_map.372 = (bf16[512,1024]{1,0:T(8,128)(2,1)}, bf16[1024,1024]{1,0:T(8,128)(2,1)}, bf16[512,128]{1,0:T(8,128)(2,1)}, bf16[512,128]{1,0:T(8,128)(2,1)}, bf1...) custom-call(s32[1]{0:T(128)} %bitcast.rank_ref.refs_0_, ...), custom_call_target="tpu_custom_call", output_to_operand_aliasing={{1}: (16, {}), {10}: (17, {})} | custom-call | tf_op jit(solution)/shard_map/pallas_call | solution.py:57
  69.9 6.7 %collective-permute-done.17.refs_4_ = bf16[256,1024]{1,0:T(8,128)(2,1)S(1)} collective-permute-done((bf16[256,1024]{1,0:T(8,128)(2,1)}, bf16[256,1024]{1,0:T(8,128)(2,1)S(1)}, u32[]{:S(2)}, u32[]{:S(2)}) %collective-permute-start.17) | collective-permute-done | bytes 524320 | tf_op jit(solution)/shard_map/ppermute | solution.py:775
  83.4 11.1 %shard_map.374 = (bf16[1024,1024]{1,0:T(8,128)(2,1)}, bf16[1024,1024]{1,0:T(8,128)(2,1)}, bf16[1024,1024]{1,0:T(8,128)(2,1)}, bf16[1024,1024]{1,0:T(8,128)(2,1)}...) custom-call(s32[1]{0:T(128)} %bitcast.rank_ref.refs_0_, ...), custom_call_target="tpu_custom_call" | custom-call | tf_op jit(solution)/shard_map/pallas_call | solution.py:57
  100.5 11.3 %shard_map.375 = (bf16[1024,1024]{1,0:T(8,128)(2,1)}, bf16[1024,1024]{1,0:T(8,128)(2,1)}, bf16[1024,1024]{1,0:T(8,128)(2,1)}, bf16[1024,1024]{1,0:T(8,128)(2,1)}...) custom-call(s32[1]{0:T(128)} %bitcast.rank_ref.refs_0_, ...), custom_call_target="tpu_custom_call", output_to_operand_aliasing={{0}: (22, {}), {1}: (23, {}), {2}: (24, {}), {3}: (25, {})} | custom-call | tf_op jit(solution)/shard_map/pallas_call | solution.py:57
  112.5 6.1 %convolution_convert_fusion.1.refs_3_ = bf16[1024,1024]{1,0:T(8,128)(2,1)} fusion(bf16[1024,1024]{1,0:T(8,128)(2,1)} %get-tuple-element.196, bf16[1024,1024]{1,0:T(8,128)(2,1)} %get-tuple-element.201), kind=kOutput, calls=%fused_computation.1 | convolution fusion | flops 2148532224 | bytes 6291456 | tf_op jit(solution)/shard_map/dot_general | solution.py:31
  118.6 3.8 %convolution_convert_fusion.2.refs_2_ = bf16[1024,1024]{1,0:T(8,128)(2,1)} fusion(bf16[1024,1024]{1,0:T(8,128)(2,1)S(1)} %copy-done.47, bf16[1024,1024]{1,0:T(8,128)(2,1)S(1)} %copy-done.45), kind=kOutput, calls=%fused_computation.2 | convolution fusion | flops 2148532224 | bytes 6291456 | tf_op jit(solution)/shard_map/dot_general | solution.py:31
  123.4 2.2 shard_map.376
  129.2 7.9 %shard_map.377 = (bf16[1024,1024]{1,0:T(8,128)(2,1)}, f32[8,1024]{1,0:T(8,128)}, f32[128,1024]{1,0:T(8,128)}, bf16[512,128]{1,0:T(8,128)(2,1)}, f32[512,128]{1,0:T(8,128)}) custom-call(s32[1]{0:T(128)} %bitcast.rank_ref.refs_0_, s32[1]{0:T(128)} %bitcast.1.side_ref.refs_1_, f32[8,1024]{1,0:T(8,128)} %get-tuple-element.164.refs_10_.refs_7_.refs_2_.refs_3_, ...), custom_call_target="tpu_custom_call" | custom-call | tf_op jit(solution)/shard_map/pallas_call | solution.py:57
  138.0 2.5 shard_map.378
  142.6 10.2 %shard_map.379 = (f32[8,1024]{1,0:T(8,128)}, bf16[1024,1024]{1,0:T(8,128)(2,1)}, f32[512,128]{1,0:T(8,128)}, f32[8,128]{1,0:T(8,128)}, bf16[2,128,1024]{2,1,0:T(8,128)(2,1)}, /*index=5*/bf16[2,128,1024]{2,1,0:T(8,128)(2,1)}) custom-call(s32[1]{0:T(128)} %bitcast.rank_ref.refs_0_, s32[1]{0:T(128)} %bitcast.1.side_ref.refs_1_, ...), custom_call_target="tpu_custom_call" | custom-call | tf_op jit(solution)/shard_map/pallas_call | solution.py:57
  156.3 2.7 shard_map.380
  162.1 7.9 %shard_map.381 = (bf16[1024,1024]{1,0:T(8,128)(2,1)}, f32[8,1024]{1,0:T(8,128)}, f32[128,1024]{1,0:T(8,128)}, bf16[512,128]{1,0:T(8,128)(2,1)}, f32[512,128]{1,0:T(8,128)}) custom-call(s32[1]{0:T(128)} %bitcast.rank_ref.refs_0_, s32[1]{0:T(128)} %bitcast.1.side_ref.refs_1_, ...), custom_call_target="tpu_custom_call", output_to_operand_aliasing={{0}: (14, {})} | custom-call | tf_op jit(solution)/shard_map/pallas_call | solution.py:57
  173.7 2.9 shard_map.382
  178.6 2.6 convolution_convert_fusion.3.refs_15_.refs_3_
  181.2 10.0 %shard_map.383 = (f32[8,1024]{1,0:T(8,128)}, bf16[1024,1024]{1,0:T(8,128)(2,1)}, f32[512,128]{1,0:T(8,128)}, f32[8,128]{1,0:T(8,128)}, bf16[2,128,1024]{2,1,0:T(8,128)(2,1)}, /*index=5*/bf16[2,128,1024]{2,1,0:T(8,128)(2,1)}) custom-call(s32[1]{0:T(128)} %bitcast.rank_ref.refs_0_, s32[1]{0:T(128)} %bitcast.1.side_ref.refs_1_, ...), custom_call_target="tpu_custom_call", output_to_operand_aliasing={{1}: (17, {})} | custom-call | tf_op jit(solution)/shard_map/pallas_call | solution.py:57
  192.2 2.7 shard_map.384
  198.7 2.0 collective-permute-done.46
  204.0 4.7 %convolution_convert_fusion = bf16[1024,1024]{1,0:T(8,128)(2,1)S(1)} fusion(bf16[1024,1024]{1,0:T(8,128)(2,1)} %shard_map.385, bf16[1024,1024]{1,0:T(8,128)(2,1)} %get-tuple-element.240), kind=kOutput, calls=%fused_computation | convolution fusion | flops 2148532224 | bytes 6291456 | tf_op jit(solution)/shard_map/dot_general | solution.py:31
  211.2 3.1 shard_map.387
  222.2 10.8 %collective-permute-done.50.refs_7_.refs_4_ = bf16[256,1024]{1,0:T(8,128)(2,1)S(1)} collective-permute-done((bf16[256,1024]{1,0:T(8,128)(2,1)}, bf16[256,1024]{1,0:T(8,128)(2,1)S(1)}, u32[]{:S(2)}, u32[]{:S(2)}) %collective-permute-start.50) | collective-permute-done | bytes 524320 | tf_op jit(solution)/shard_map/ppermute | solution.py:807
  235.0 3.7 %collective-permute-done.44.refs_6_ = bf16[96,1024]{1,0:T(8,128)(2,1)S(1)} collective-permute-done((bf16[96,1024]{1,0:T(8,128)(2,1)}, bf16[96,1024]{1,0:T(8,128)(2,1)S(1)}, u32[]{:S(2)}, u32[]{:S(2)}) %collective-permute-start.44) | collective-permute-done | bytes 196640 | tf_op jit(solution)/shard_map/ppermute | solution.py:807
  240.1 3.4 shard_map.389
  245.7 10.5 %collective-permute-done.52.refs_5_ = bf16[208,1024]{1,0:T(8,128)(2,1)S(1)} collective-permute-done((bf16[208,1024]{1,0:T(8,128)(2,1)}, bf16[208,1024]{1,0:T(8,128)(2,1)S(1)}, u32[]{:S(2)}, u32[]{:S(2)}) %collective-permute-start.52) | collective-permute-done | bytes 426016 | tf_op jit(solution)/shard_map/ppermute | solution.py:807
  258.5 3.5 shard_map.390
  268.3 1.7 collective-permute-start.64
  270.0 5.7 %collective-permute-done.59.refs_8_.refs_10_ = bf16[128,1024]{1,0:T(8,128)(2,1)S(1)} collective-permute-done((bf16[128,1024]{1,0:T(8,128)(2,1)S(1)}, bf16[128,1024]{1,0:T(8,128)(2,1)S(1)}, u32[]{:S(2)}, u32[]{:S(2)}) %collective-permute-start.59) | collective-permute-done | bytes 262176 | tf_op jit(solution)/shard_map/ppermute | solution.py:807
  275.7 3.0 collective-permute-done.58.refs_7_.refs_9_
  278.7 2.9 collective-permute-done.57.refs_6_
  282.3 3.5 shard_map.391
  289.0 1.8 shard_map.392.refs_7_
  290.8 4.4 %collective-permute-done.60.refs_5_ = bf16[208,1024]{1,0:T(8,128)(2,1)S(1)} collective-permute-done((bf16[208,1024]{1,0:T(8,128)(2,1)}, bf16[208,1024]{1,0:T(8,128)(2,1)S(1)}, u32[]{:S(2)}, u32[]{:S(2)}) %collective-permute-start.60) | collective-permute-done | bytes 426016 | tf_op jit(solution)/shard_map/ppermute | solution.py:807
  296.7 3.5 shard_map.393
  302.1 3.1 collective-permute-done.66
  310.2 3.9 %shard_map.394 = (f32[1024,1024]{1,0:T(8,128)}, f32[256,4096]{1,0:T(8,128)}) custom-call(s32[1]{0:T(128)} %bitcast.rank_ref.refs_0_, s32[1]{0:T(128)} %bitcast.14.refs_1_, bf16[256,1024]{1,0:T(8,128)(2,1)S(1)} %constant_dynamic-update-slice_fusion.refs_2_, bf16[256,1024]{1,0:T(8,128)(2,1)S(1)} %copy-done.20, bf16[256,1024]{1,0:T(8,128)(2,1)S(1)} %copy-done.16, ...), custom_call_target="tpu_custom_call" | custom-call | tf_op jit(solution)/shard_map/pallas_call | solution.py:57
  314.1 6.0 %shard_map.395 = (bf16[2,2,128,1024]{3,2,1,0:T(8,128)(2,1)}, bf16[2,2,128,1024]{3,2,1,0:T(8,128)(2,1)}) custom-call(s32[1]{0:T(128)} %bitcast.rank_ref.refs_0_, s32[1]{0:T(128)} %bitcast.1.side_ref.refs_1_, bf16[1024,1024]{1,0:T(8,128)(2,1)} %get-tuple-element.191.refs_2_, bf16[1024,1024]{1,0:T(8,128)(2,1)} %refs_3_.1, bf16[208,1024]{1,0:T(8,128)(2,1)} %copy-done.2, ...), custom_call_target="tpu_custom_call" | custom-call | tf_op jit(solution)/shard_map/pallas_call | solution.py:57
  324.0 9.3 %collective-permute-done.74.refs_4_ = bf16[208,1024]{1,0:T(8,128)(2,1)S(1)} collective-permute-done((bf16[208,1024]{1,0:T(8,128)(2,1)S(1)}, bf16[208,1024]{1,0:T(8,128)(2,1)S(1)}, u32[]{:S(2)}, u32[]{:S(2)}) %collective-permute-start.74) | collective-permute-done | bytes 426016 | tf_op jit(solution)/shard_map/ppermute | solution.py:807
  336.8 6.9 %collective-permute-done.75.refs_5_ = bf16[208,1024]{1,0:T(8,128)(2,1)S(1)} collective-permute-done((bf16[208,1024]{1,0:T(8,128)(2,1)S(1)}, bf16[208,1024]{1,0:T(8,128)(2,1)S(1)}, u32[]{:S(2)}, u32[]{:S(2)}) %collective-permute-start.75) | collective-permute-done | bytes 426016 | tf_op jit(solution)/shard_map/ppermute | solution.py:807
  345.9 1.7 collective-permute-done.71.refs_5_
  348.6 1.7 collective-permute-done.77.refs_10_
  351.4 5.6 %shard_map.399 = (f32[448,256]{1,0:T(8,128)}, f32[20,256]{1,0:T(8,128)}, f32[20,256]{1,0:T(8,128)}, f32[448,256]{1,0:T(8,128)}, f32[448,256]{1,0:T(8,128)}, /*in...) custom-call(s32[1]{0:T(128)} %bitcast.rank_ref.refs_0_, ...), custom_call_target="tpu_custom_call" | custom-call | tf_op jit(solution)/shard_map/pallas_call | solution.py:57
  (391 shorter events, 110.4 us)
Async XLA Ops:
  7.8 11.5 %collective-permute-start.1 = (bf16[1024,128]{1,0:T(8,128)(2,1)}, bf16[1024,128]{1,0:T(8,128)(2,1)S(1)}, u32[]{:S(2)}, u32[]{:S(2)}) collective-permute-start(bf16[1024,128]{1,0:T(8,128)(2,1)} %get-tuple-element.160), channel_id=1, source_target_pairs={{0,3},{1,2},{2,1},{3,0},{4,7},{5,6},{6,5},{7,4},{8,11},{9,10},{10,... | collective-permute-start | bytes 786440 | tf_op jit(solution)/shard_map/ppermute | solution.py:775
  7.8 28.8 %collective-permute-start.5 = (bf16[1024,256]{1,0:T(8,128)(2,1)}, bf16[1024,256]{1,0:T(8,128)(2,1)S(1)}, u32[]{:S(2)}, u32[]{:S(2)}) collective-permute-start(bf16[1024,256]{1,0:T(8,128)(2,1)} %get-tuple-element.163), channel_id=1, source_target_pairs={{0,1},{1,0},{2,3},{3,2},{4,5},{5,4},{6,7},{7,6},{8,9},{9,8},{10,11... | collective-permute-start | bytes 1572872 | tf_op jit(solution)/shard_map/ppermute | solution.py:775
  23.4 12.6 %collective-permute-start.7 = (bf16[1024,128]{1,0:T(8,128)(2,1)}, bf16[1024,128]{1,0:T(8,128)(2,1)S(1)}, u32[]{:S(2)}, u32[]{:S(2)}) collective-permute-start(bf16[1024,128]{1,0:T(8,128)(2,1)} %copy-done.70), channel_id=1, source_target_pairs={{0,4},{4,0},{8,12},{12,8},{16,20},{20,16},{24,28},{28,24},{1,5},{5... | collective-permute-start | bytes 786440 | tf_op jit(solution)/shard_map/ppermute | solution.py:780
  28.9 19.3 %collective-permute-start.12 = (bf16[128,1024]{1,0:T(8,128)(2,1)S(1)}, bf16[128,1024]{1,0:T(8,128)(2,1)S(1)}, u32[]{:S(2)}, u32[]{:S(2)}) collective-permute-start(bf16[128,1024]{1,0:T(8,128)(2,1)S(1)} %copy-done.109), channel_id=1, source_target_pairs={{0,3},{1,2},{2,1},{3,0},{4,7},{5,6},{6,5},{7,4},{8,11},{9,10},{10,... | collective-permute-start | bytes 786440 | tf_op jit(solution)/shard_map/ppermute | solution.py:775
  31.3 17.6 %collective-permute-start.11 = (bf16[128,1024]{1,0:T(8,128)(2,1)}, bf16[128,1024]{1,0:T(8,128)(2,1)S(1)}, u32[]{:S(2)}, u32[]{:S(2)}) collective-permute-start(bf16[128,1024]{1,0:T(8,128)(2,1)} %get-tuple-element.170), channel_id=1, source_target_pairs={{0,2},{1,3},{2,0},{3,1},{4,6},{5,7},{6,4},{7,5},{8,10},{9,11},{10,... | collective-permute-start | bytes 786440 | tf_op jit(solution)/shard_map/ppermute | solution.py:775
  35.9 13.7 %collective-permute-start.9 = (bf16[128,1024]{1,0:T(8,128)(2,1)}, bf16[128,1024]{1,0:T(8,128)(2,1)S(1)}, u32[]{:S(2)}, u32[]{:S(2)}) collective-permute-start(bf16[128,1024]{1,0:T(8,128)(2,1)} %get-tuple-element.165), channel_id=1, source_target_pairs={{0,2},{1,3},{2,0},{3,1},{4,6},{5,7},{6,4},{7,5},{8,10},{9,11},{10,... | collective-permute-start | bytes 786440 | tf_op jit(solution)/shard_map/ppermute | solution.py:775
  36.6 13.1 %collective-permute-start.8 = (bf16[128,1024]{1,0:T(8,128)(2,1)}, bf16[128,1024]{1,0:T(8,128)(2,1)S(1)}, u32[]{:S(2)}, u32[]{:S(2)}) collective-permute-start(bf16[128,1024]{1,0:T(8,128)(2,1)} %get-tuple-element.165), channel_id=1, source_target_pairs={{0,1},{1,0},{2,3},{3,2},{4,5},{5,4},{6,7},{7,6},{8,9},{9,8},{10,11... | collective-permute-start | bytes 786440 | tf_op jit(solution)/shard_map/ppermute | solution.py:775
  51.4 17.5 %collective-permute-start.16 = (bf16[2,128,1024]{2,1,0:T(8,128)(2,1)S(1)}, bf16[2,128,1024]{2,1,0:T(8,128)(2,1)S(1)}, u32[]{:S(2)}, u32[]{:S(2)}) collective-permute-start(bf16[2,128,1024]{2,1,0:T(8,128)(2,1)S(1)} %bitcast.38), channel_id=1, source_target_pairs={{0,2},{1,3},{2,0},{3,1},{4,6},{5,7},{6,4},{7,5},{8,10},{9,11},{10,... | collective-permute-start | bytes 1572872 | tf_op jit(solution)/shard_map/ppermute | solution.py:775
  54.2 22.5 %collective-permute-start.17 = (bf16[256,1024]{1,0:T(8,128)(2,1)}, bf16[256,1024]{1,0:T(8,128)(2,1)S(1)}, u32[]{:S(2)}, u32[]{:S(2)}) collective-permute-start(bf16[256,1024]{1,0:T(8,128)(2,1)} %add_convert_fusion.4.refs_14_.refs_15_.refs_3_), channel_id=1, source_target_pairs={{0,2},{1,3},{2,0},{3,1},{4,6},{5,7},{6,4},{7,5},{8,10},{9,11},{10,... | collective-permute-start | bytes 1572872 | tf_op jit(solution)/shard_map/ppermute | solution.py:775
  55.7 13.3 %collective-permute-start.15 = (bf16[128,1024]{1,0:T(8,128)(2,1)S(1)}, bf16[128,1024]{1,0:T(8,128)(2,1)S(1)}, u32[]{:S(2)}, u32[]{:S(2)}) collective-permute-start(bf16[128,1024]{1,0:T(8,128)(2,1)S(1)} %copy-done.51), channel_id=1, source_target_pairs={{0,4},{4,0},{8,12},{12,8},{16,20},{20,16},{24,28},{28,24},{1,5},{5... | collective-permute-start | bytes 786440 | tf_op jit(solution)/shard_map/ppermute | solution.py:780
  57.2 12.8 %collective-permute-start.14 = (bf16[128,1024]{1,0:T(8,128)(2,1)S(1)}, bf16[128,1024]{1,0:T(8,128)(2,1)S(1)}, u32[]{:S(2)}, u32[]{:S(2)}) collective-permute-start(bf16[128,1024]{1,0:T(8,128)(2,1)S(1)} %copy-done.53), channel_id=1, source_target_pairs={{0,4},{4,0},{8,12},{12,8},{16,20},{20,16},{24,28},{28,24},{1,5},{5... | collective-permute-start | bytes 786440 | tf_op jit(solution)/shard_map/ppermute | solution.py:780
  81.0 14.2 %collective-permute-start.19 = (bf16[256,1024]{1,0:T(8,128)(2,1)S(1)}, bf16[256,1024]{1,0:T(8,128)(2,1)S(1)}, u32[]{:S(2)}, u32[]{:S(2)}) collective-permute-start(bf16[256,1024]{1,0:T(8,128)(2,1)S(1)} %add_convert_fusion.3.refs_20_.refs_21_.refs_3_), channel_id=1, source_target_pairs={{0,2},{1,3},{2,0},{3,1},{4,6},{5,7},{6,4},{7,5},{8,10},{9,11},{10,... | collective-permute-start | bytes 1572872 | tf_op jit(solution)/shard_map/ppermute | solution.py:775
  98.0 20.6 %collective-permute-start.34 = (bf16[256,1024]{1,0:T(8,128)(2,1)S(1)}, bf16[256,1024]{1,0:T(8,128)(2,1)S(1)}, u32[]{:S(2)}, u32[]{:S(2)}) collective-permute-start(bf16[256,1024]{1,0:T(8,128)(2,1)S(1)} %add_convert_fusion.2.refs_20_.refs_21_.refs_6_), channel_id=1, source_target_pairs={{0,2},{1,3},{2,0},{3,1},{4,6},{5,7},{6,4},{7,5},{8,10},{9,11},{10,... | collective-permute-start | bytes 1572872 | tf_op jit(solution)/shard_map/ppermute | solution.py:775
  99.5 28.8 %collective-permute-start.35 = (bf16[256,1024]{1,0:T(8,128)(2,1)S(1)}, bf16[256,1024]{1,0:T(8,128)(2,1)S(1)}, u32[]{:S(2)}, u32[]{:S(2)}) collective-permute-start(bf16[256,1024]{1,0:T(8,128)(2,1)S(1)} %add_convert_fusion.2.refs_20_.refs_21_.refs_6_), channel_id=1, source_target_pairs={{0,1},{1,0},{2,3},{3,2},{4,5},{5,4},{6,7},{7,6},{8,9},{9,8},{10,11... | collective-permute-start | bytes 1572872 | tf_op jit(solution)/shard_map/ppermute | solution.py:775
  111.8 10.6 %collective-permute-start.28 = (bf16[256,1024]{1,0:T(8,128)(2,1)}, bf16[256,1024]{1,0:T(8,128)(2,1)S(1)}, u32[]{:S(2)}, u32[]{:S(2)}) collective-permute-start(bf16[256,1024]{1,0:T(8,128)(2,1)} %get-tuple-element.198), channel_id=1, source_target_pairs={{0,1},{1,0},{2,3},{3,2},{4,5},{5,4},{6,7},{7,6},{8,9},{9,8},{10,11... | collective-permute-start | bytes 1572872 | tf_op jit(solution)/shard_map/ppermute | solution.py:775
  125.6 11.5 %collective-permute-start.32 = (bf16[128,1024]{1,0:T(8,128)(2,1)}, bf16[128,1024]{1,0:T(8,128)(2,1)S(1)}, u32[]{:S(2)}, u32[]{:S(2)}) collective-permute-start(bf16[128,1024]{1,0:T(8,128)(2,1)} %get-tuple-element.202.refs_13_), channel_id=1, source_target_pairs={{0,8},{8,16},{16,24},{24,28},{28,20},{20,12},{12,4},{4,0},{1,9},{9... | collective-permute-start | bytes 786440 | tf_op jit(solution)/shard_map/ppermute | solution.py:807
  127.7 25.1 %collective-permute-start.29 = (bf16[256,1024]{1,0:T(8,128)(2,1)S(1)}, bf16[256,1024]{1,0:T(8,128)(2,1)S(1)}, u32[]{:S(2)}, u32[]{:S(2)}) collective-permute-start(bf16[256,1024]{1,0:T(8,128)(2,1)S(1)} %copy-done.55), channel_id=1, source_target_pairs={{0,2},{1,3},{2,0},{3,1},{4,6},{5,7},{6,4},{7,5},{8,10},{9,11},{10,... | collective-permute-start | bytes 1572872 | tf_op jit(solution)/shard_map/ppermute | solution.py:775
  140.5 13.7 %collective-permute-start.37 = (bf16[256,1024]{1,0:T(8,128)(2,1)}, bf16[256,1024]{1,0:T(8,128)(2,1)S(1)}, u32[]{:S(2)}, u32[]{:S(2)}) collective-permute-start(bf16[256,1024]{1,0:T(8,128)(2,1)} %get-tuple-element.209.refs_15_), channel_id=1, source_target_pairs={{0,8},{8,16},{16,24},{24,28},{28,20},{20,12},{12,4},{4,0},{1,9},{9... | collective-permute-start | bytes 1572872 | tf_op jit(solution)/shard_map/ppermute | solution.py:807
  142.1 13.4 %collective-permute-start.38 = (bf16[256,1024]{1,0:T(8,128)(2,1)}, bf16[256,1024]{1,0:T(8,128)(2,1)S(1)}, u32[]{:S(2)}, u32[]{:S(2)}) collective-permute-start(bf16[256,1024]{1,0:T(8,128)(2,1)} %get-tuple-element.210), channel_id=1, source_target_pairs={{0,4},{8,0},{16,8},{24,16},{28,24},{20,28},{12,20},{4,12},{1,5},{9... | collective-permute-start | bytes 1572872 | tf_op jit(solution)/shard_map/ppermute | solution.py:807
  142.6 18.6 %collective-permute-start.30 = (bf16[256,1024]{1,0:T(8,128)(2,1)S(1)}, bf16[256,1024]{1,0:T(8,128)(2,1)S(1)}, u32[]{:S(2)}, u32[]{:S(2)}) collective-permute-start(bf16[256,1024]{1,0:T(8,128)(2,1)S(1)} %copy-done.55), channel_id=1, source_target_pairs={{0,1},{1,0},{2,3},{3,2},{4,5},{5,4},{6,7},{7,6},{8,9},{9,8},{10,11... | collective-permute-start | bytes 1572872 | tf_op jit(solution)/shard_map/ppermute | solution.py:775
  159.0 12.5 %collective-permute-start.39 = (bf16[256,1024]{1,0:T(8,128)(2,1)}, bf16[256,1024]{1,0:T(8,128)(2,1)S(1)}, u32[]{:S(2)}, u32[]{:S(2)}) collective-permute-start(bf16[256,1024]{1,0:T(8,128)(2,1)} %get-tuple-element.221.refs_13_), channel_id=1, source_target_pairs={{0,8},{8,16},{16,24},{24,28},{28,20},{20,12},{12,4},{4,0},{1,9},{9... | collective-permute-start | bytes 1572872 | tf_op jit(solution)/shard_map/ppermute | solution.py:807
  160.7 12.2 %collective-permute-start.40 = (bf16[256,1024]{1,0:T(8,128)(2,1)}, bf16[256,1024]{1,0:T(8,128)(2,1)S(1)}, u32[]{:S(2)}, u32[]{:S(2)}) collective-permute-start(bf16[256,1024]{1,0:T(8,128)(2,1)} %get-tuple-element.233), channel_id=1, source_target_pairs={{0,4},{8,0},{16,8},{24,16},{28,24},{20,28},{12,20},{4,12},{1,5},{9... | collective-permute-start | bytes 1572872 | tf_op jit(solution)/shard_map/ppermute | solution.py:807
  176.5 14.7 %collective-permute-start.41 = (bf16[256,1024]{1,0:T(8,128)(2,1)}, bf16[256,1024]{1,0:T(8,128)(2,1)S(1)}, u32[]{:S(2)}, u32[]{:S(2)}) collective-permute-start(bf16[256,1024]{1,0:T(8,128)(2,1)} %get-tuple-element.234.refs_16_), channel_id=1, source_target_pairs={{0,8},{8,16},{16,24},{24,28},{28,20},{20,12},{12,4},{4,0},{1,9},{9... | collective-permute-start | bytes 1572872 | tf_op jit(solution)/shard_map/ppermute | solution.py:807
  178.2 13.1 %collective-permute-start.42 = (bf16[256,1024]{1,0:T(8,128)(2,1)}, bf16[256,1024]{1,0:T(8,128)(2,1)S(1)}, u32[]{:S(2)}, u32[]{:S(2)}) collective-permute-start(bf16[256,1024]{1,0:T(8,128)(2,1)} %get-tuple-element.237), channel_id=1, source_target_pairs={{0,4},{8,0},{16,8},{24,16},{28,24},{20,28},{12,20},{4,12},{1,5},{9... | collective-permute-start | bytes 1572872 | tf_op jit(solution)/shard_map/ppermute | solution.py:807
  201.9 13.9 %collective-permute-start.48 = (bf16[256,1024]{1,0:T(8,128)(2,1)S(1)}, bf16[256,1024]{1,0:T(8,128)(2,1)S(1)}, u32[]{:S(2)}, u32[]{:S(2)}) collective-permute-start(bf16[256,1024]{1,0:T(8,128)(2,1)S(1)} %constant_dynamic-update-slice_fusion.refs_2_), channel_id=1, source_target_pairs={{0,8},{8,16},{16,24},{24,28},{28,20},{20,12},{12,4},{4,0},{1,9},{9... | collective-permute-start | bytes 1572872 | tf_op jit(solution)/shard_map/ppermute | solution.py:807
  203.5 13.7 %collective-permute-start.49 = (bf16[256,1024]{1,0:T(8,128)(2,1)S(1)}, bf16[256,1024]{1,0:T(8,128)(2,1)S(1)}, u32[]{:S(2)}, u32[]{:S(2)}) collective-permute-start(bf16[256,1024]{1,0:T(8,128)(2,1)S(1)} %constant_dynamic-update-slice_fusion.refs_2_), channel_id=1, source_target_pairs={{0,4},{8,0},{16,8},{24,16},{28,24},{20,28},{12,20},{4,12},{1,5},{9... | collective-permute-start | bytes 1572872 | tf_op jit(solution)/shard_map/ppermute | solution.py:807
  217.9 15.1 %collective-permute-start.50 = (bf16[256,1024]{1,0:T(8,128)(2,1)}, bf16[256,1024]{1,0:T(8,128)(2,1)S(1)}, u32[]{:S(2)}, u32[]{:S(2)}) collective-permute-start(bf16[256,1024]{1,0:T(8,128)(2,1)} %shard_map.388.refs_3_), channel_id=1, source_target_pairs={{0,8},{8,16},{16,24},{24,28},{28,20},{20,12},{12,4},{4,0},{1,9},{9... | collective-permute-start | bytes 1572872 | tf_op jit(solution)/shard_map/ppermute | solution.py:807
  219.4 15.1 %collective-permute-start.51 = (bf16[256,1024]{1,0:T(8,128)(2,1)}, bf16[256,1024]{1,0:T(8,128)(2,1)S(1)}, u32[]{:S(2)}, u32[]{:S(2)}) collective-permute-start(bf16[256,1024]{1,0:T(8,128)(2,1)} %copy-done.13), channel_id=1, source_target_pairs={{0,4},{8,0},{16,8},{24,16},{28,24},{20,28},{12,20},{4,12},{1,5},{9... | collective-permute-start | bytes 1572872 | tf_op jit(solution)/shard_map/ppermute | solution.py:807
  220.0 24.9 %collective-permute-start.62 = (bf16[2,128,1024]{2,1,0:T(8,128)(2,1)S(1)}, bf16[2,128,1024]{2,1,0:T(8,128)(2,1)S(1)}, u32[]{:S(2)}, u32[]{:S(2)}) collective-permute-start(bf16[2,128,1024]{2,1,0:T(8,128)(2,1)S(1)} %copy-done.106), channel_id=1, source_target_pairs={{0,1},{1,0},{2,3},{3,2},{4,5},{5,4},{6,7},{7,6},{8,9},{9,8},{10,11... | collective-permute-start | bytes 1572872 | tf_op jit(solution)/shard_map/ppermute | solution.py:775
  220.0 18.8 %collective-permute-start.44 = (bf16[96,1024]{1,0:T(8,128)(2,1)}, bf16[96,1024]{1,0:T(8,128)(2,1)S(1)}, u32[]{:S(2)}, u32[]{:S(2)}) collective-permute-start(bf16[96,1024]{1,0:T(8,128)(2,1)} %get-tuple-element.250), channel_id=1, source_target_pairs={{0,4},{8,0},{16,8},{24,16},{28,24},{20,28},{12,20},{4,12},{1,5},{9... | collective-permute-start | bytes 589832 | tf_op jit(solution)/shard_map/ppermute | solution.py:807
  220.6 18.1 %collective-permute-start.43 = (bf16[112,1024]{1,0:T(8,128)(2,1)}, bf16[112,1024]{1,0:T(8,128)(2,1)S(1)}, u32[]{:S(2)}, u32[]{:S(2)}) collective-permute-start(bf16[112,1024]{1,0:T(8,128)(2,1)} %get-tuple-element.249.refs_1_.refs_9_), channel_id=1, source_target_pairs={{0,8},{8,16},{16,24},{24,28},{28,20},{20,12},{12,4},{4,0},{1,9},{9... | collective-permute-start | bytes 688136 | tf_op jit(solution)/shard_map/ppermute | solution.py:807
  233.0 23.7 %collective-permute-start.54 = (bf16[256,1024]{1,0:T(8,128)(2,1)S(1)}, bf16[256,1024]{1,0:T(8,128)(2,1)S(1)}, u32[]{:S(2)}, u32[]{:S(2)}) collective-permute-start(bf16[256,1024]{1,0:T(8,128)(2,1)S(1)} %collective-permute-done.50.refs_7_.refs_4_), channel_id=1, source_target_pairs={{0,8},{8,16},{16,24},{24,28},{28,20},{20,12},{12,4},{4,0},{1,9},{9... | collective-permute-start | bytes 1572872 | tf_op jit(solution)/shard_map/ppermute | solution.py:807
  234.5 22.2 %collective-permute-start.55 = (bf16[256,1024]{1,0:T(8,128)(2,1)S(1)}, bf16[256,1024]{1,0:T(8,128)(2,1)S(1)}, u32[]{:S(2)}, u32[]{:S(2)}) collective-permute-start(bf16[256,1024]{1,0:T(8,128)(2,1)S(1)} %collective-permute-done.51.refs_8_.refs_7_), channel_id=1, source_target_pairs={{0,4},{8,0},{16,8},{24,16},{28,24},{20,28},{12,20},{4,12},{1,5},{9... | collective-permute-start | bytes 1572872 | tf_op jit(solution)/shard_map/ppermute | solution.py:807
  238.7 29.4 %collective-permute-start.63 = (bf16[2,128,1024]{2,1,0:T(8,128)(2,1)S(1)}, bf16[2,128,1024]{2,1,0:T(8,128)(2,1)S(1)}, u32[]{:S(2)}, u32[]{:S(2)}) collective-permute-start(bf16[2,128,1024]{2,1,0:T(8,128)(2,1)S(1)} %copy-done.107), channel_id=1, source_target_pairs={{0,1},{1,0},{2,3},{3,2},{4,5},{5,4},{6,7},{7,6},{8,9},{9,8},{10,11... | collective-permute-start | bytes 1572872 | tf_op jit(solution)/shard_map/ppermute | solution.py:775
  243.5 12.7 %collective-permute-start.52 = (bf16[208,1024]{1,0:T(8,128)(2,1)}, bf16[208,1024]{1,0:T(8,128)(2,1)S(1)}, u32[]{:S(2)}, u32[]{:S(2)}) collective-permute-start(bf16[208,1024]{1,0:T(8,128)(2,1)} %get-tuple-element.255.refs_9_), channel_id=1, source_target_pairs={{0,8},{8,16},{16,24},{24,28},{28,20},{20,12},{12,4},{4,0},{1,9},{9... | collective-permute-start | bytes 1277960 | tf_op jit(solution)/shard_map/ppermute | solution.py:807
  244.8 11.9 %collective-permute-start.53 = (bf16[208,1024]{1,0:T(8,128)(2,1)}, bf16[208,1024]{1,0:T(8,128)(2,1)S(1)}, u32[]{:S(2)}, u32[]{:S(2)}) collective-permute-start(bf16[208,1024]{1,0:T(8,128)(2,1)} %get-tuple-element.256), channel_id=1, source_target_pairs={{0,4},{8,0},{16,8},{24,16},{28,24},{20,28},{12,20},{4,12},{1,5},{9... | collective-permute-start | bytes 1277960 | tf_op jit(solution)/shard_map/ppermute | solution.py:807
  262.0 16.7 %collective-permute-start.56 = (bf16[208,1024]{1,0:T(8,128)(2,1)}, bf16[208,1024]{1,0:T(8,128)(2,1)S(1)}, u32[]{:S(2)}, u32[]{:S(2)}) collective-permute-start(bf16[208,1024]{1,0:T(8,128)(2,1)} %get-tuple-element.257), channel_id=1, source_target_pairs={{0,8},{8,16},{16,24},{24,28},{28,20},{20,12},{12,4},{4,0},{1,9},{9... | collective-permute-start | bytes 1277960 | tf_op jit(solution)/shard_map/ppermute | solution.py:807
  264.2 14.4 %collective-permute-start.58 = (bf16[128,1024]{1,0:T(8,128)(2,1)S(1)}, bf16[128,1024]{1,0:T(8,128)(2,1)S(1)}, u32[]{:S(2)}, u32[]{:S(2)}) collective-permute-start(bf16[128,1024]{1,0:T(8,128)(2,1)S(1)} %slice.30), channel_id=1, source_target_pairs={{0,8},{8,16},{16,24},{24,28},{28,20},{20,12},{12,4},{4,0},{1,9},{9... | collective-permute-start | bytes 786440 | tf_op jit(solution)/shard_map/ppermute | solution.py:807
  267.4 14.2 %collective-permute-start.57 = (bf16[208,1024]{1,0:T(8,128)(2,1)}, bf16[208,1024]{1,0:T(8,128)(2,1)S(1)}, u32[]{:S(2)}, u32[]{:S(2)}) collective-permute-start(bf16[208,1024]{1,0:T(8,128)(2,1)} %get-tuple-element.258), channel_id=1, source_target_pairs={{0,4},{8,0},{16,8},{24,16},{28,24},{20,28},{12,20},{4,12},{1,5},{9... | collective-permute-start | bytes 1277960 | tf_op jit(solution)/shard_map/ppermute | solution.py:807
  268.3 19.6 %collective-permute-start.64 = (bf16[2,128,1024]{2,1,0:T(8,128)(2,1)S(1)}, bf16[2,128,1024]{2,1,0:T(8,128)(2,1)S(1)}, u32[]{:S(2)}, u32[]{:S(2)}) collective-permute-start(bf16[2,128,1024]{2,1,0:T(8,128)(2,1)S(1)} %pad_maximum_fusion.1), channel_id=1, source_target_pairs={{0,2},{1,3},{2,0},{3,1},{4,6},{5,7},{6,4},{7,5},{8,10},{9,11},{10,... | collective-permute-start | bytes 1572872 | tf_op jit(solution)/shard_map/ppermute | solution.py:775
  307.1 12.9 %collective-permute-start.68 = (bf16[208,1024]{1,0:T(8,128)(2,1)S(1)}, bf16[208,1024]{1,0:T(8,128)(2,1)S(1)}, u32[]{:S(2)}, u32[]{:S(2)}) collective-permute-start(bf16[208,1024]{1,0:T(8,128)(2,1)S(1)} %pad_maximum_fusion.2.refs_11_.refs_4_.refs_2_), channel_id=1, source_target_pairs={{0,8},{8,16},{16,24},{24,28},{28,20},{20,12},{12,4},{4,0},{1,9},{9... | collective-permute-start | bytes 1277960 | tf_op jit(solution)/shard_map/ppermute | solution.py:807
  308.0 12.1 %collective-permute-start.69 = (bf16[208,1024]{1,0:T(8,128)(2,1)S(1)}, bf16[208,1024]{1,0:T(8,128)(2,1)S(1)}, u32[]{:S(2)}, u32[]{:S(2)}) collective-permute-start(bf16[208,1024]{1,0:T(8,128)(2,1)S(1)} %pad_maximum_fusion.2.refs_11_.refs_4_.refs_2_), channel_id=1, source_target_pairs={{0,4},{8,0},{16,8},{24,16},{28,24},{20,28},{12,20},{4,12},{1,5},{9... | collective-permute-start | bytes 1277960 | tf_op jit(solution)/shard_map/ppermute | solution.py:807
  321.0 14.3 %collective-permute-start.70 = (bf16[2,2,128,1024]{3,2,1,0:T(8,128)(2,1)}, bf16[2,2,128,1024]{3,2,1,0:T(8,128)(2,1)S(1)}, u32[]{:S(2)}, u32[]{:S(2)}) collective-permute-start(bf16[2,2,128,1024]{3,2,1,0:T(8,128)(2,1)} %shard_map.397), channel_id=1, source_target_pairs={{0,1},{1,0},{2,3},{3,2},{4,5},{5,4},{6,7},{7,6},{8,9},{9,8},{10,11... | collective-permute-start | bytes 3145736 | tf_op jit(solution)/shard_map/ppermute | solution.py:775
  321.9 11.3 %collective-permute-start.74 = (bf16[208,1024]{1,0:T(8,128)(2,1)S(1)}, bf16[208,1024]{1,0:T(8,128)(2,1)S(1)}, u32[]{:S(2)}, u32[]{:S(2)}) collective-permute-start(bf16[208,1024]{1,0:T(8,128)(2,1)S(1)} %copy-done.6), channel_id=1, source_target_pairs={{0,8},{8,16},{16,24},{24,28},{28,20},{20,12},{12,4},{4,0},{1,9},{9... | collective-permute-start | bytes 1277960 | tf_op jit(solution)/shard_map/ppermute | solution.py:807
  322.8 11.3 %collective-permute-start.72 = (bf16[208,1024]{1,0:T(8,128)(2,1)S(1)}, bf16[208,1024]{1,0:T(8,128)(2,1)S(1)}, u32[]{:S(2)}, u32[]{:S(2)}) collective-permute-start(bf16[208,1024]{1,0:T(8,128)(2,1)S(1)} %copy-done.22), channel_id=1, source_target_pairs={{0,4},{8,0},{16,8},{24,16},{28,24},{20,28},{12,20},{4,12},{1,5},{9... | collective-permute-start | bytes 1277960 | tf_op jit(solution)/shard_map/ppermute | solution.py:807
  333.3 10.4 %collective-permute-start.75 = (bf16[208,1024]{1,0:T(8,128)(2,1)S(1)}, bf16[208,1024]{1,0:T(8,128)(2,1)S(1)}, u32[]{:S(2)}, u32[]{:S(2)}) collective-permute-start(bf16[208,1024]{1,0:T(8,128)(2,1)S(1)} %collective-permute-done.74.refs_4_), channel_id=1, source_target_pairs={{0,8},{8,16},{16,24},{24,28},{28,20},{20,12},{12,4},{4,0},{1,9},{9... | collective-permute-start | bytes 1277960 | tf_op jit(solution)/shard_map/ppermute | solution.py:807
  334.1 10.5 %collective-permute-start.73 = (bf16[208,1024]{1,0:T(8,128)(2,1)S(1)}, bf16[208,1024]{1,0:T(8,128)(2,1)S(1)}, u32[]{:S(2)}, u32[]{:S(2)}) collective-permute-start(bf16[208,1024]{1,0:T(8,128)(2,1)S(1)} %collective-permute-done.72.refs_7_), channel_id=1, source_target_pairs={{0,4},{8,0},{16,8},{24,16},{28,24},{20,28},{12,20},{4,12},{1,5},{9... | collective-permute-start | bytes 1277960 | tf_op jit(solution)/shard_map/ppermute | solution.py:807
  335.5 12.0 %collective-permute-start.71 = (bf16[2,128,1024]{2,1,0:T(8,128)(2,1)S(1)}, bf16[2,128,1024]{2,1,0:T(8,128)(2,1)S(1)}, u32[]{:S(2)}, u32[]{:S(2)}) collective-permute-start(bf16[2,128,1024]{2,1,0:T(8,128)(2,1)S(1)} %fusion.3), channel_id=1, source_target_pairs={{0,2},{1,3},{2,0},{3,1},{4,6},{5,7},{6,4},{7,5},{8,10},{9,11},{10,... | collective-permute-start | bytes 1572872 | tf_op jit(solution)/shard_map/ppermute | solution.py:775
  (141 other events, 815.8 us)
where the time goes:
time: 365 us; the launch traced here: 357 us
  Pallas kernels  132 us (36%)
  waiting for transfers between devices  103 us (28%)
  starting transfers between devices  61.8 us (17%)
  local copies, waits for them, and re-layouts  29.7 us (8%)
  matrix products  17.5 us (5%)
  other arithmetic  11 us (3%)
    pallas_call x25, Pallas kernels, call(): pl.pallas_call(body if deps else kernel, out_shape=out_shapes, in_specs=i...  132 us
    ppermute x32, waiting for transfers between devices, pass_on(): return lax.ppermute(value, 'dp', pairs)  67.1 us
    ppermute x32, starting transfers between devices, pass_on(): return lax.ppermute(value, 'dp', pairs)  33.3 us
    ppermute x42, waiting for transfers between devices, flip_shard(): return lax.ppermute(value, 'shard', [(s, s ^ bit) for s in range(H)])  29.9 us
    unnamed x226, local copies, waits for them, and re-layouts  27.8 us
    ppermute x42, starting transfers between devices, flip_shard(): return lax.ppermute(value, 'shard', [(s, s ^ bit) for s in range(H)])  24.5 us
    dot_general x5, matrix products, mm(): return lax.dot_general(a, b, dims, preferred_element_type=f32)  17.5 us
  transfers between devices with their start and end apart: 78, of which 37 were waited for; matrix products, arithmetic and copies ran while one was open for 8% of the time, Pallas kernels for 32%

commit v1 on v0

--- a/solution.py
+++ b/solution.py
@@ -593,10 +593,14 @@
 
 
 def output_kernel(rank_ref, side_ref, vec_ref, keep_ref, got_ref, far_ref, *refs):
-    y_ref = refs[-1]
+    *refs, y_hbm, done_ref, y_ref, sems = refs
+    done_ref[...] = jnp.zeros(done_ref.shape, f32)
     for m in range(y_ref.shape[0]):
         total = refs[m][...] + keep_ref[0, m].astype(f32) + got_ref[0, m].astype(f32)
         y_ref[m, 0] = (total + far_ref[m].astype(f32) + vec_ref[4:5, :]).astype(bf16)
+    copies = Copies(sems)
+    copies.start(y_ref, y_hbm)
+    copies.finish()
 
 
 def input_kernel(rank_ref, side_ref, x_ref, vec_ref, far_ref, *refs):
@@ -710,7 +714,8 @@
 
 
 def ffn_grads_kernel(split, rank_ref, pos_ref, *refs):
-    parts, (o_hbm, i_hbm, held, o_ref, i_ref, sems) = refs[:9], refs[9:]
+    parts, (o_hbm, i_hbm, done_ref, held, o_ref, i_ref, sems) = refs[:9], refs[9:]
+    done_ref[...] = jnp.zeros(done_ref.shape, f32)
     copies = Copies(sems)
     load_ring(copies, pos_ref[0], split, parts, held)
     rows = D // RING
@@ -873,7 +878,7 @@
     def kernel(fn, outs, args, second=side, **kwargs):
         deps = [*kwargs.pop("deps", ()), *([] if token[0] is me else [token[0]])]
         res = call(fn, outs, [me, second, *args], deps=deps, **kwargs)
-        token[0] = res[0]
+        token[0] = min(res, key=lambda r: r.size)
         return res
 
     packs = kernel(
@@ -1079,14 +1084,15 @@
 
         def gather(self, piece):
             self.parts = [[piece], [piece]]
+            self.cuts = []
             self.pass_parts()
 
         def pass_parts(self):
             for way, parts in zip((1, -1), self.parts):
                 value = parts[-1]
                 if len(parts) == 4:
-                    cut = (lambda v: v[: self.split]) if way == 1 else (lambda v: v[self.split :])
-                    value = step(cut, value)
+                    value = value[: self.split] if way == 1 else value[self.split :]
+                    self.cuts.append(value)
                 parts.append(pass_on(value, way))
 
         def result(self):
@@ -1187,32 +1193,22 @@
     came = lambda i: [p[i] for p in ffn_ring.parts]
     both_ways = ffn_ring.parts
     both_ways[0][1] = gate(both_ways[0][1], [pack_ring.sent, both_ways[1][1]])
-    for i in range(1, 4):
-        ffn_ring.pass_parts()
-        pack_ring.step(deps=came(i + 1))
+    ffn_ring.pass_parts()
+    pack_ring.step()
+    pack_ring.step(deps=came(2))
+    ffn_ring.pass_parts()
+    pack_ring.step()
     gx_all = kernel(
         input_kernel,
         [out((micro, 1, own, D), f32)],
         [x_own, vec, gx_far]
         + [a for m in range(micro) for a in (branch[m][2], back[m][4], gx_got[m])],
     )[0]
-    piece, *parts = pack_ring.step()
+    ffn_ring.pass_parts()
+    piece, *parts = pack_ring.step(deps=ffn_ring.cuts)
+    parts[0] = gate(parts[0], came(4))
     pack_piece = jnp.concatenate([jnp.concatenate(turned(parts), axis=1), piece])
     pack_ring.gather(pack_piece)
-    g_out, g_in = kernel(
-        functools.partial(ffn_grads_kernel, ffn_ring.split),
-        [Far(out((FF // H, D), f32)), Far(out((quarter, FF), f32))],
-        [Far(p) for p in ffn_ring.result()],
-        second=place,
-        scratch=[
-            pltpu.VMEM((RING, ffn_ring.total, D), bf16),
-            pltpu.VMEM((FF // H, D), f32),
-            pltpu.VMEM((quarter, FF), f32),
-        ],
-        copies=25,
-        vmem=40,
-        deps=[pack_piece],
-    )
     ways = pack_ring.parts
     sides = out((2, micro, own, D), bf16)
     keep, send = kernel(
@@ -1224,16 +1220,33 @@
         vmem=56,
         deps=[pack_piece],
     )
-    ways[0][1] = gate(ways[0][1], [g_out, keep, ways[1][1]])
+    ways[0][1] = gate(ways[0][1], [keep, ways[1][1]])
     got = flip_shard(gate(send, [ways[0][1]]), 1)
     far = flip_shard(add(keep[1], got[1]), 2)
     pack_ring.pass_parts()
+    g_out, g_in, done = kernel(
+        functools.partial(ffn_grads_kernel, ffn_ring.split),
+        [Far(out((FF // H, D), f32)), Far(out((quarter, FF), f32)), out((8, LANE), f32)],
+        [Far(p) for p in ffn_ring.result()],
+        second=place,
+        scratch=[
+            pltpu.VMEM((RING, ffn_ring.total, D), bf16),
+            pltpu.VMEM((FF // H, D), f32),
+            pltpu.VMEM((quarter, FF), f32),
+        ],
+        copies=25,
+        vmem=60,
+        deps=[ways[0][1]],
+    )
+    ways[0][2] = gate(ways[0][2], [done, ways[1][2]])
     pack_ring.pass_parts()
     pack_ring.pass_parts()
     y_all = kernel(
         output_kernel,
-        [out((micro, 1, own, D), bf16)],
+        [Far(out((micro, 1, own, D), bf16)), out((8, LANE), f32)],
         [vec, keep, got, far] + [ffn[m][6] for m in range(micro)],
+        scratch=[pltpu.VMEM((micro, 1, own, D), bf16)],
+        copies=1,
     )[0]
     res = kernel(
         functools.partial(pack_grads_kernel, pack_ring.split),

time: 365 us -> 354 us (0.970)
  waiting for transfers between devices: 103 us -> 90.2 us
    ppermute x32, waiting for transfers between devices: 67.1 us -> 58.1 us  [pass_on(): return lax.ppermute(value, 'dp', pairs)]
    ppermute x42, waiting for transfers between devices: 29.9 us -> 26.2 us  [flip_shard(): return lax.ppermute(value, 'shard', [(s, s ^ bit) for s in range(H)])]
    unnamed x226 -> x227, local copies, waits for them, and re-layouts: 27.8 us -> 30.8 us
  transfers between devices with their start and end apart: 78 -> 78, of which waited for: 37 -> 40; matrix products, arithmetic and copies ran while one was open for 8% -> 9% of each run, Pallas kernels for 32% -> 35%
where the time goes in v1:
time: 354 us; the launch traced here: 347 us
  Pallas kernels  135 us (38%)
  waiting for transfers between devices  90.2 us (25%)
  starting transfers between devices  61.4 us (17%)
  local copies, waits for them, and re-layouts  31.4 us (9%)
  matrix products  17 us (5%)
  other arithmetic  9.92 us (3%)
    pallas_call x25, Pallas kernels, call(): pl.pallas_call(body if deps else kernel, out_shape=out_shapes, in_specs=i...  135 us
    ppermute x32, waiting for transfers between devices, pass_on(): return lax.ppermute(value, 'dp', pairs)  58.1 us
    ppermute x32, starting transfers between devices, pass_on(): return lax.ppermute(value, 'dp', pairs)  33.3 us
    unnamed x227, local copies, waits for them, and re-layouts  30.8 us
    ppermute x42, waiting for transfers between devices, flip_shard(): return lax.ppermute(value, 'shard', [(s, s ^ bit) for s in range(H)])  26.2 us
    ppermute x42, starting transfers between devices, flip_shard(): return lax.ppermute(value, 'shard', [(s, s ^ bit) for s in range(H)])  24.1 us
    dot_general x5, matrix products, mm(): return lax.dot_general(a, b, dims, preferred_element_type=f32)  17 us
  transfers between devices with their start and end apart: 78, of which 40 were waited for; matrix products, arithmetic and copies ran while one was open for 9% of the time, Pallas kernels for 35%

profile of v1, /device:TPU:0, one launch (start us, length us, event | category | flops | bytes accessed | tf_op | source)
XLA Modules:
  0.0 346.9 jit_solution(2558343281090743147)
XLA Ops:
  0.7 4.1 %shard_map.366 = (bf16[1024,256]{1,0:T(8,128)(2,1)}, bf16[1024,256]{1,0:T(8,128)(2,1)}, bf16[1024,128]{1,0:T(8,128)(2,1)}, bf16[1024,128]{1,0:T(8,128)(2,1)}, f3...) custom-call(s32[1]{0:T(128)} %bitcast.rank_ref.refs_0_, ...), custom_call_target="tpu_custom_call" | custom-call | tf_op jit(solution)/shard_map/pallas_call | solution.py:57
  4.7 3.0 collective-permute-start
  8.0 4.1 %fusion.1 = (bf16[512,512]{1,0:T(8,128)(2,1)S(1)}, bf16[512,512]{1,0:T(8,128)(2,1)S(1)}) fusion(f32[512]{0:T(512)S(1)} %multiply_exponential_fusion, f32[512]{0:T(512)S(1)} %subtract_convert_fusion), kind=kLoop, calls=%fused_computation.8 | loop fusion | flops 786432 | bytes 1052672 | tf_op jit(solution)/shard_map/convert
  15.1 4.2 %collective-permute-done.1.refs_2_.refs_10_ = bf16[1024,128]{1,0:T(8,128)(2,1)S(1)} collective-permute-done((bf16[1024,128]{1,0:T(8,128)(2,1)}, bf16[1024,128]{1,0:T(8,128)(2,1)S(1)}, u32[]{:S(2)}, u32[]{:S(2)}) %collective-permute-start.1) | collective-permute-done | bytes 262176 | tf_op jit(solution)/shard_map/ppermute | solution.py:780
  23.9 4.9 %collective-permute-done.3.refs_4_ = bf16[128,1024]{1,0:T(8,128)(2,1)S(1)} collective-permute-done((bf16[128,1024]{1,0:T(8,128)(2,1)}, bf16[128,1024]{1,0:T(8,128)(2,1)S(1)}, u32[]{:S(2)}, u32[]{:S(2)}) %collective-permute-start.3) | collective-permute-done | bytes 262176 | tf_op jit(solution)/shard_map/ppermute | solution.py:780
  28.9 1.9 collective-permute-start.12
  31.5 4.4 %collective-permute-done.7.refs_12_ = bf16[1024,128]{1,0:T(8,128)(2,1)S(1)} collective-permute-done((bf16[1024,128]{1,0:T(8,128)(2,1)}, bf16[1024,128]{1,0:T(8,128)(2,1)S(1)}, u32[]{:S(2)}, u32[]{:S(2)}) %collective-permute-start.7) | collective-permute-done | bytes 262176 | tf_op jit(solution)/shard_map/ppermute | solution.py:785
  37.4 10.8 %shard_map.368 = (bf16[512,1024]{1,0:T(8,128)(2,1)}, bf16[1024,1024]{1,0:T(8,128)(2,1)}, bf16[512,128]{1,0:T(8,128)(2,1)}, bf16[512,128]{1,0:T(8,128)(2,1)}, bf1...) custom-call(s32[1]{0:T(128)} %bitcast.rank_ref.refs_0_, ...), custom_call_target="tpu_custom_call" | custom-call | tf_op jit(solution)/shard_map/pallas_call | solution.py:57
  58.4 10.5 %shard_map.372 = (bf16[512,1024]{1,0:T(8,128)(2,1)}, bf16[1024,1024]{1,0:T(8,128)(2,1)}, bf16[512,128]{1,0:T(8,128)(2,1)}, bf16[512,128]{1,0:T(8,128)(2,1)}, bf1...) custom-call(s32[1]{0:T(128)} %bitcast.rank_ref.refs_0_, ...), custom_call_target="tpu_custom_call", output_to_operand_aliasing={{1}: (16, {}), {10}: (17, {})} | custom-call | tf_op jit(solution)/shard_map/pallas_call | solution.py:57
  70.0 6.7 %collective-permute-done.17.refs_4_ = bf16[256,1024]{1,0:T(8,128)(2,1)S(1)} collective-permute-done((bf16[256,1024]{1,0:T(8,128)(2,1)}, bf16[256,1024]{1,0:T(8,128)(2,1)S(1)}, u32[]{:S(2)}, u32[]{:S(2)}) %collective-permute-start.17) | collective-permute-done | bytes 524320 | tf_op jit(solution)/shard_map/ppermute | solution.py:780
  83.5 11.2 %shard_map.374 = (bf16[1024,1024]{1,0:T(8,128)(2,1)}, bf16[1024,1024]{1,0:T(8,128)(2,1)}, bf16[1024,1024]{1,0:T(8,128)(2,1)}, bf16[1024,1024]{1,0:T(8,128)(2,1)}...) custom-call(s32[1]{0:T(128)} %bitcast.rank_ref.refs_0_, ...), custom_call_target="tpu_custom_call" | custom-call | tf_op jit(solution)/shard_map/pallas_call | solution.py:57
  100.7 11.3 %shard_map.375 = (bf16[1024,1024]{1,0:T(8,128)(2,1)}, bf16[1024,1024]{1,0:T(8,128)(2,1)}, bf16[1024,1024]{1,0:T(8,128)(2,1)}, bf16[1024,1024]{1,0:T(8,128)(2,1)}...) custom-call(s32[1]{0:T(128)} %bitcast.rank_ref.refs_0_, ...), custom_call_target="tpu_custom_call", output_to_operand_aliasing={{0}: (22, {}), {1}: (23, {}), {2}: (24, {}), {3}: (25, {})} | custom-call | tf_op jit(solution)/shard_map/pallas_call | solution.py:57
  112.7 6.1 %convolution_convert_fusion.1.refs_3_ = bf16[1024,1024]{1,0:T(8,128)(2,1)} fusion(bf16[1024,1024]{1,0:T(8,128)(2,1)} %get-tuple-element.202, bf16[1024,1024]{1,0:T(8,128)(2,1)} %get-tuple-element.203), kind=kOutput, calls=%fused_computation.1 | convolution fusion | flops 2148532224 | bytes 6291456 | tf_op jit(solution)/shard_map/dot_general | solution.py:31
  118.9 3.8 %convolution_convert_fusion.2.refs_2_ = bf16[1024,1024]{1,0:T(8,128)(2,1)} fusion(bf16[1024,1024]{1,0:T(8,128)(2,1)S(1)} %copy-done.34, bf16[1024,1024]{1,0:T(8,128)(2,1)S(1)} %copy-done.33), kind=kOutput, calls=%fused_computation.2 | convolution fusion | flops 2148532224 | bytes 6291456 | tf_op jit(solution)/shard_map/dot_general | solution.py:31
  123.6 2.2 shard_map.376
  129.5 7.9 %shard_map.377 = (bf16[1024,1024]{1,0:T(8,128)(2,1)}, f32[8,1024]{1,0:T(8,128)}, f32[128,1024]{1,0:T(8,128)}, bf16[512,128]{1,0:T(8,128)(2,1)}, f32[512,128]{1,0:T(8,128)}) custom-call(s32[1]{0:T(128)} %bitcast.rank_ref.refs_0_, s32[1]{0:T(128)} %bitcast.1.side_ref.refs_1_, f32[8,1024]{1,0:T(8,128)} %get-tuple-element.163.refs_10_.refs_7_.refs_2_.refs_3_, ...), custom_call_target="tpu_custom_call" | custom-call | tf_op jit(solution)/shard_map/pallas_call | solution.py:57
  138.2 2.6 shard_map.378
  140.8 1.6 collective-permute-start.37
  142.9 10.2 %shard_map.379 = (f32[8,1024]{1,0:T(8,128)}, bf16[1024,1024]{1,0:T(8,128)(2,1)}, f32[512,128]{1,0:T(8,128)}, f32[8,128]{1,0:T(8,128)}, bf16[2,128,1024]{2,1,0:T(8,128)(2,1)}, /*index=5*/bf16[2,128,1024]{2,1,0:T(8,128)(2,1)}) custom-call(s32[1]{0:T(128)} %bitcast.rank_ref.refs_0_, s32[1]{0:T(128)} %bitcast.1.side_ref.refs_1_, ...), custom_call_target="tpu_custom_call" | custom-call | tf_op jit(solution)/shard_map/pallas_call | solution.py:57
  156.6 2.7 shard_map.380
  162.4 7.9 %shard_map.381 = (bf16[1024,1024]{1,0:T(8,128)(2,1)}, f32[8,1024]{1,0:T(8,128)}, f32[128,1024]{1,0:T(8,128)}, bf16[512,128]{1,0:T(8,128)(2,1)}, f32[512,128]{1,0:T(8,128)}) custom-call(s32[1]{0:T(128)} %bitcast.rank_ref.refs_0_, s32[1]{0:T(128)} %bitcast.1.side_ref.refs_1_, ...), custom_call_target="tpu_custom_call", output_to_operand_aliasing={{0}: (14, {})} | custom-call | tf_op jit(solution)/shard_map/pallas_call | solution.py:57
  174.0 2.9 shard_map.382
  178.9 2.7 convolution_convert_fusion.3.refs_15_.refs_3_
  181.7 10.0 %shard_map.383 = (f32[8,1024]{1,0:T(8,128)}, bf16[1024,1024]{1,0:T(8,128)(2,1)}, f32[512,128]{1,0:T(8,128)}, f32[8,128]{1,0:T(8,128)}, bf16[2,128,1024]{2,1,0:T(8,128)(2,1)}, /*index=5*/bf16[2,128,1024]{2,1,0:T(8,128)(2,1)}) custom-call(s32[1]{0:T(128)} %bitcast.rank_ref.refs_0_, s32[1]{0:T(128)} %bitcast.1.side_ref.refs_1_, ...), custom_call_target="tpu_custom_call", output_to_operand_aliasing={{1}: (17, {})} | custom-call | tf_op jit(solution)/shard_map/pallas_call | solution.py:57
  192.6 2.7 shard_map.384
  195.3 1.7 constant_dynamic-update-slice_fusion.4
  206.3 4.1 %convolution_convert_fusion = bf16[1024,1024]{1,0:T(8,128)(2,1)S(1)} fusion(bf16[1024,1024]{1,0:T(8,128)(2,1)} %shard_map.385, bf16[1024,1024]{1,0:T(8,128)(2,1)S(1)} %copy-done.46), kind=kOutput, calls=%fused_computation | convolution fusion | flops 2148532224 | bytes 6291456 | tf_op jit(solution)/shard_map/dot_general | solution.py:31
  212.9 3.1 shard_map.387
  218.3 2.3 collective-permute-done.51.refs_2_.refs_6_
  221.4 1.7 collective-permute-start.52
  225.2 3.4 shard_map.388
  228.6 1.8 collective-permute-start.45
  230.8 13.0 %collective-permute-done.45.refs_5_ = bf16[208,1024]{1,0:T(8,128)(2,1)S(1)} collective-permute-done((bf16[208,1024]{1,0:T(8,128)(2,1)}, bf16[208,1024]{1,0:T(8,128)(2,1)S(1)}, u32[]{:S(2)}, u32[]{:S(2)}) %collective-permute-start.45) | collective-permute-done | bytes 426016 | tf_op jit(solution)/shard_map/ppermute | solution.py:812
  245.8 3.5 %shard_map.390 = (bf16[208,1024]{1,0:T(8,128)(2,1)}, bf16[208,1024]{1,0:T(8,128)(2,1)}) custom-call(s32[1]{0:T(128)} %bitcast.rank_ref.refs_0_, s32[1]{0:T(128)} %bitcast.14.refs_1_, bf16[1024,1024]{1,0:T(8,128)(2,1)} %copy-done.32, bf16[640,1024]{1,0:T(8,128)(2,1)} %convolution_convert_fusion.3.refs_15_.refs_3_, f32[8,8,1024]{2,1,0:T(8,128)} %copy-done.1, ...), custom_call_target="tpu_custom_call" | custom-call | tf_op jit(solution)/shard_map/pallas_call | solution.py:57
  254.8 7.6 %collective-permute-done.54.refs_5_ = bf16[208,1024]{1,0:T(8,128)(2,1)S(1)} collective-permute-done((bf16[208,1024]{1,0:T(8,128)(2,1)}, bf16[208,1024]{1,0:T(8,128)(2,1)S(1)}, u32[]{:S(2)}, u32[]{:S(2)}) %collective-permute-start.54) | collective-permute-done | bytes 426016 | tf_op jit(solution)/shard_map/ppermute | solution.py:812
  264.6 3.5 %shard_map.391 = (bf16[208,1024]{1,0:T(8,128)(2,1)}, bf16[208,1024]{1,0:T(8,128)(2,1)}) custom-call(s32[1]{0:T(128)} %bitcast.rank_ref.refs_0_, s32[1]{0:T(128)} %bitcast.14.refs_1_, bf16[1024,1024]{1,0:T(8,128)(2,1)} %copy-done.32, bf16[640,1024]{1,0:T(8,128)(2,1)} %convolution_convert_fusion.3.refs_15_.refs_3_, f32[8,8,1024]{2,1,0:T(8,128)} %copy-done.1, ...), custom_call_target="tpu_custom_call" | custom-call | tf_op jit(solution)/shard_map/pallas_call | solution.py:57
  270.2 3.4 collective-permute-done.58.refs_5_
  276.8 1.8 shard_map.392.refs_9_
  278.6 3.9 %collective-permute-done.56.refs_5_ = bf16[208,1024]{1,0:T(8,128)(2,1)S(1)} collective-permute-done((bf16[208,1024]{1,0:T(8,128)(2,1)}, bf16[208,1024]{1,0:T(8,128)(2,1)S(1)}, u32[]{:S(2)}, u32[]{:S(2)}) %collective-permute-start.56) | collective-permute-done | bytes 426016 | tf_op jit(solution)/shard_map/ppermute | solution.py:812
  284.8 3.5 %shard_map.393 = (bf16[80,1024]{1,0:T(8,128)(2,1)}, bf16[128,256]{1,0:T(8,128)(2,1)}, bf16[128,256]{1,0:T(8,128)(2,1)}, bf16[128,256]{1,0:T(8,128)(2,1)}, bf16[128,256]{1,0:T(8,128)(2,1)}) custom-call(s32[1]{0:T(128)} %bitcast.rank_ref.refs_0_, s32[1]{0:T(128)} %bitcast.14.refs_1_, bf16[1024,1024]{1,0:T(8,128)(2,1)} %copy-done.32, ...), custom_call_target="tpu_custom_call" | custom-call | tf_op jit(solution)/shard_map/pallas_call | solution.py:57
  295.1 1.6 collective-permute-start.68
  297.2 6.0 %shard_map.395 = (bf16[2,2,128,1024]{3,2,1,0:T(8,128)(2,1)}, bf16[2,2,128,1024]{3,2,1,0:T(8,128)(2,1)}) custom-call(s32[1]{0:T(128)} %bitcast.rank_ref.refs_0_, s32[1]{0:T(128)} %bitcast.1.side_ref.refs_1_, bf16[1024,1024]{1,0:T(8,128)(2,1)} %get-tuple-element.192.refs_2_, bf16[1024,1024]{1,0:T(8,128)(2,1)} %refs_3_.1, bf16[208,1024]{1,0:T(8,128)(2,1)} %copy-done.6, ...), custom_call_target="tpu_custom_call" | custom-call | tf_op jit(solution)/shard_map/pallas_call | solution.py:57
  303.2 3.9 %collective-permute-done.68.refs_0_ = bf16[208,1024]{1,0:T(8,128)(2,1)S(1)} collective-permute-done((bf16[208,1024]{1,0:T(8,128)(2,1)S(1)}, bf16[208,1024]{1,0:T(8,128)(2,1)S(1)}, u32[]{:S(2)}, u32[]{:S(2)}) %collective-permute-start.68) | collective-permute-done | bytes 426016 | tf_op jit(solution)/shard_map/ppermute | solution.py:812
  312.2 6.3 %shard_map.398 = (f32[1024,1024]{1,0:T(8,128)}, f32[256,4096]{1,0:T(8,128)}, f32[8,128]{1,0:T(8,128)}) custom-call(s32[1]{0:T(128)} %bitcast.rank_ref.refs_0_, s32[1]{0:T(128)} %bitcast.14.refs_1_, bf16[256,1024]{1,0:T(8,128)(2,1)} %constant_dynamic-update-slice_fusion.refs_2_, bf16[256,1024]{1,0:T(8,128)(2,1)} %shard_map.389.refs_3_, ...), custom_call_target="tpu_custom_call" | custom-call | tf_op jit(solution)/shard_map/pallas_call | solution.py:57
  318.5 3.0 collective-permute-done.72.refs_0_
  326.6 7.1 %collective-permute-done.74.refs_5_ = bf16[208,1024]{1,0:T(8,128)(2,1)S(1)} collective-permute-done((bf16[208,1024]{1,0:T(8,128)(2,1)}, bf16[208,1024]{1,0:T(8,128)(2,1)S(1)}, u32[]{:S(2)}, u32[]{:S(2)}) %collective-permute-start.74) | collective-permute-done | bytes 426016 | tf_op jit(solution)/shard_map/ppermute | solution.py:812
  338.3 2.4 collective-permute-done.77.refs_10_
  340.8 5.7 %shard_map.401 = (f32[448,256]{1,0:T(8,128)}, f32[20,256]{1,0:T(8,128)}, f32[20,256]{1,0:T(8,128)}, f32[448,256]{1,0:T(8,128)}, f32[448,256]{1,0:T(8,128)}, /*in...) custom-call(s32[1]{0:T(128)} %bitcast.rank_ref.refs_0_, ...), custom_call_target="tpu_custom_call" | custom-call | tf_op jit(solution)/shard_map/pallas_call | solution.py:57
  (394 shorter events, 110.3 us)
Async XLA Ops:
  7.8 11.5 %collective-permute-start.1 = (bf16[1024,128]{1,0:T(8,128)(2,1)}, bf16[1024,128]{1,0:T(8,128)(2,1)S(1)}, u32[]{:S(2)}, u32[]{:S(2)}) collective-permute-start(bf16[1024,128]{1,0:T(8,128)(2,1)} %get-tuple-element.159), channel_id=1, source_target_pairs={{0,3},{1,2},{2,1},{3,0},{4,7},{5,6},{6,5},{7,4},{8,11},{9,10},{10,... | collective-permute-start | bytes 786440 | tf_op jit(solution)/shard_map/ppermute | solution.py:780
  7.8 28.8 %collective-permute-start.5 = (bf16[1024,256]{1,0:T(8,128)(2,1)}, bf16[1024,256]{1,0:T(8,128)(2,1)S(1)}, u32[]{:S(2)}, u32[]{:S(2)}) collective-permute-start(bf16[1024,256]{1,0:T(8,128)(2,1)} %get-tuple-element.162), channel_id=1, source_target_pairs={{0,1},{1,0},{2,3},{3,2},{4,5},{5,4},{6,7},{7,6},{8,9},{9,8},{10,11... | collective-permute-start | bytes 1572872 | tf_op jit(solution)/shard_map/ppermute | solution.py:780
  23.4 12.6 %collective-permute-start.7 = (bf16[1024,128]{1,0:T(8,128)(2,1)}, bf16[1024,128]{1,0:T(8,128)(2,1)S(1)}, u32[]{:S(2)}, u32[]{:S(2)}) collective-permute-start(bf16[1024,128]{1,0:T(8,128)(2,1)} %copy-done.69), channel_id=1, source_target_pairs={{0,4},{4,0},{8,12},{12,8},{16,20},{20,16},{24,28},{28,24},{1,5},{5... | collective-permute-start | bytes 786440 | tf_op jit(solution)/shard_map/ppermute | solution.py:785
  28.9 19.3 %collective-permute-start.12 = (bf16[128,1024]{1,0:T(8,128)(2,1)S(1)}, bf16[128,1024]{1,0:T(8,128)(2,1)S(1)}, u32[]{:S(2)}, u32[]{:S(2)}) collective-permute-start(bf16[128,1024]{1,0:T(8,128)(2,1)S(1)} %copy-done.109), channel_id=1, source_target_pairs={{0,3},{1,2},{2,1},{3,0},{4,7},{5,6},{6,5},{7,4},{8,11},{9,10},{10,... | collective-permute-start | bytes 786440 | tf_op jit(solution)/shard_map/ppermute | solution.py:780
  31.3 17.7 %collective-permute-start.11 = (bf16[128,1024]{1,0:T(8,128)(2,1)S(1)}, bf16[128,1024]{1,0:T(8,128)(2,1)S(1)}, u32[]{:S(2)}, u32[]{:S(2)}) collective-permute-start(bf16[128,1024]{1,0:T(8,128)(2,1)S(1)} %copy-done.108), channel_id=1, source_target_pairs={{0,2},{1,3},{2,0},{3,1},{4,6},{5,7},{6,4},{7,5},{8,10},{9,11},{10,... | collective-permute-start | bytes 786440 | tf_op jit(solution)/shard_map/ppermute | solution.py:780
  35.9 13.7 %collective-permute-start.9 = (bf16[128,1024]{1,0:T(8,128)(2,1)S(1)}, bf16[128,1024]{1,0:T(8,128)(2,1)S(1)}, u32[]{:S(2)}, u32[]{:S(2)}) collective-permute-start(bf16[128,1024]{1,0:T(8,128)(2,1)S(1)} %copy-done.107), channel_id=1, source_target_pairs={{0,2},{1,3},{2,0},{3,1},{4,6},{5,7},{6,4},{7,5},{8,10},{9,11},{10,... | collective-permute-start | bytes 786440 | tf_op jit(solution)/shard_map/ppermute | solution.py:780
  36.6 13.1 %collective-permute-start.8 = (bf16[128,1024]{1,0:T(8,128)(2,1)S(1)}, bf16[128,1024]{1,0:T(8,128)(2,1)S(1)}, u32[]{:S(2)}, u32[]{:S(2)}) collective-permute-start(bf16[128,1024]{1,0:T(8,128)(2,1)S(1)} %copy-done.107), channel_id=1, source_target_pairs={{0,1},{1,0},{2,3},{3,2},{4,5},{5,4},{6,7},{7,6},{8,9},{9,8},{10,11... | collective-permute-start | bytes 786440 | tf_op jit(solution)/shard_map/ppermute | solution.py:780
  51.5 17.5 %collective-permute-start.16 = (bf16[2,128,1024]{2,1,0:T(8,128)(2,1)S(1)}, bf16[2,128,1024]{2,1,0:T(8,128)(2,1)S(1)}, u32[]{:S(2)}, u32[]{:S(2)}) collective-permute-start(bf16[2,128,1024]{2,1,0:T(8,128)(2,1)S(1)} %bitcast.38), channel_id=1, source_target_pairs={{0,2},{1,3},{2,0},{3,1},{4,6},{5,7},{6,4},{7,5},{8,10},{9,11},{10,... | collective-permute-start | bytes 1572872 | tf_op jit(solution)/shard_map/ppermute | solution.py:780
  54.2 22.5 %collective-permute-start.17 = (bf16[256,1024]{1,0:T(8,128)(2,1)}, bf16[256,1024]{1,0:T(8,128)(2,1)S(1)}, u32[]{:S(2)}, u32[]{:S(2)}) collective-permute-start(bf16[256,1024]{1,0:T(8,128)(2,1)} %add_convert_fusion.4.refs_14_.refs_15_.refs_3_), channel_id=1, source_target_pairs={{0,2},{1,3},{2,0},{3,1},{4,6},{5,7},{6,4},{7,5},{8,10},{9,11},{10,... | collective-permute-start | bytes 1572872 | tf_op jit(solution)/shard_map/ppermute | solution.py:780
  55.7 13.2 %collective-permute-start.15 = (bf16[128,1024]{1,0:T(8,128)(2,1)S(1)}, bf16[128,1024]{1,0:T(8,128)(2,1)S(1)}, u32[]{:S(2)}, u32[]{:S(2)}) collective-permute-start(bf16[128,1024]{1,0:T(8,128)(2,1)S(1)} %copy-done.38), channel_id=1, source_target_pairs={{0,4},{4,0},{8,12},{12,8},{16,20},{20,16},{24,28},{28,24},{1,5},{5... | collective-permute-start | bytes 786440 | tf_op jit(solution)/shard_map/ppermute | solution.py:785
  57.2 12.8 %collective-permute-start.14 = (bf16[128,1024]{1,0:T(8,128)(2,1)S(1)}, bf16[128,1024]{1,0:T(8,128)(2,1)S(1)}, u32[]{:S(2)}, u32[]{:S(2)}) collective-permute-start(bf16[128,1024]{1,0:T(8,128)(2,1)S(1)} %copy-done.40), channel_id=1, source_target_pairs={{0,4},{4,0},{8,12},{12,8},{16,20},{20,16},{24,28},{28,24},{1,5},{5... | collective-permute-start | bytes 786440 | tf_op jit(solution)/shard_map/ppermute | solution.py:785
  81.1 14.2 %collective-permute-start.19 = (bf16[256,1024]{1,0:T(8,128)(2,1)S(1)}, bf16[256,1024]{1,0:T(8,128)(2,1)S(1)}, u32[]{:S(2)}, u32[]{:S(2)}) collective-permute-start(bf16[256,1024]{1,0:T(8,128)(2,1)S(1)} %add_convert_fusion.3.refs_20_.refs_21_.refs_3_), channel_id=1, source_target_pairs={{0,2},{1,3},{2,0},{3,1},{4,6},{5,7},{6,4},{7,5},{8,10},{9,11},{10,... | collective-permute-start | bytes 1572872 | tf_op jit(solution)/shard_map/ppermute | solution.py:780
  98.1 20.7 %collective-permute-start.34 = (bf16[256,1024]{1,0:T(8,128)(2,1)S(1)}, bf16[256,1024]{1,0:T(8,128)(2,1)S(1)}, u32[]{:S(2)}, u32[]{:S(2)}) collective-permute-start(bf16[256,1024]{1,0:T(8,128)(2,1)S(1)} %add_convert_fusion.2.refs_20_.refs_21_.refs_6_), channel_id=1, source_target_pairs={{0,2},{1,3},{2,0},{3,1},{4,6},{5,7},{6,4},{7,5},{8,10},{9,11},{10,... | collective-permute-start | bytes 1572872 | tf_op jit(solution)/shard_map/ppermute | solution.py:780
  99.6 28.9 %collective-permute-start.35 = (bf16[256,1024]{1,0:T(8,128)(2,1)S(1)}, bf16[256,1024]{1,0:T(8,128)(2,1)S(1)}, u32[]{:S(2)}, u32[]{:S(2)}) collective-permute-start(bf16[256,1024]{1,0:T(8,128)(2,1)S(1)} %add_convert_fusion.2.refs_20_.refs_21_.refs_6_), channel_id=1, source_target_pairs={{0,1},{1,0},{2,3},{3,2},{4,5},{5,4},{6,7},{7,6},{8,9},{9,8},{10,11... | collective-permute-start | bytes 1572872 | tf_op jit(solution)/shard_map/ppermute | solution.py:780
  112.0 10.6 %collective-permute-start.28 = (bf16[256,1024]{1,0:T(8,128)(2,1)}, bf16[256,1024]{1,0:T(8,128)(2,1)S(1)}, u32[]{:S(2)}, u32[]{:S(2)}) collective-permute-start(bf16[256,1024]{1,0:T(8,128)(2,1)} %get-tuple-element.199), channel_id=1, source_target_pairs={{0,1},{1,0},{2,3},{3,2},{4,5},{5,4},{6,7},{7,6},{8,9},{9,8},{10,11... | collective-permute-start | bytes 1572872 | tf_op jit(solution)/shard_map/ppermute | solution.py:780
  125.9 11.6 %collective-permute-start.32 = (bf16[128,1024]{1,0:T(8,128)(2,1)}, bf16[128,1024]{1,0:T(8,128)(2,1)S(1)}, u32[]{:S(2)}, u32[]{:S(2)}) collective-permute-start(bf16[128,1024]{1,0:T(8,128)(2,1)} %get-tuple-element.204.refs_13_), channel_id=1, source_target_pairs={{0,8},{8,16},{16,24},{24,28},{28,20},{20,12},{12,4},{4,0},{1,9},{9... | collective-permute-start | bytes 786440 | tf_op jit(solution)/shard_map/ppermute | solution.py:812
  127.9 25.1 %collective-permute-start.29 = (bf16[256,1024]{1,0:T(8,128)(2,1)S(1)}, bf16[256,1024]{1,0:T(8,128)(2,1)S(1)}, u32[]{:S(2)}, u32[]{:S(2)}) collective-permute-start(bf16[256,1024]{1,0:T(8,128)(2,1)S(1)} %copy-done.42), channel_id=1, source_target_pairs={{0,2},{1,3},{2,0},{3,1},{4,6},{5,7},{6,4},{7,5},{8,10},{9,11},{10,... | collective-permute-start | bytes 1572872 | tf_op jit(solution)/shard_map/ppermute | solution.py:780
  140.8 13.7 %collective-permute-start.37 = (bf16[256,1024]{1,0:T(8,128)(2,1)}, bf16[256,1024]{1,0:T(8,128)(2,1)S(1)}, u32[]{:S(2)}, u32[]{:S(2)}) collective-permute-start(bf16[256,1024]{1,0:T(8,128)(2,1)} %get-tuple-element.211.refs_15_), channel_id=1, source_target_pairs={{0,8},{8,16},{16,24},{24,28},{28,20},{20,12},{12,4},{4,0},{1,9},{9... | collective-permute-start | bytes 1572872 | tf_op jit(solution)/shard_map/ppermute | solution.py:812
  142.4 13.4 %collective-permute-start.38 = (bf16[256,1024]{1,0:T(8,128)(2,1)}, bf16[256,1024]{1,0:T(8,128)(2,1)S(1)}, u32[]{:S(2)}, u32[]{:S(2)}) collective-permute-start(bf16[256,1024]{1,0:T(8,128)(2,1)} %get-tuple-element.212), channel_id=1, source_target_pairs={{0,4},{8,0},{16,8},{24,16},{28,24},{20,28},{12,20},{4,12},{1,5},{9... | collective-permute-start | bytes 1572872 | tf_op jit(solution)/shard_map/ppermute | solution.py:812
  142.9 18.6 %collective-permute-start.30 = (bf16[256,1024]{1,0:T(8,128)(2,1)S(1)}, bf16[256,1024]{1,0:T(8,128)(2,1)S(1)}, u32[]{:S(2)}, u32[]{:S(2)}) collective-permute-start(bf16[256,1024]{1,0:T(8,128)(2,1)S(1)} %copy-done.42), channel_id=1, source_target_pairs={{0,1},{1,0},{2,3},{3,2},{4,5},{5,4},{6,7},{7,6},{8,9},{9,8},{10,11... | collective-permute-start | bytes 1572872 | tf_op jit(solution)/shard_map/ppermute | solution.py:780
  159.4 12.5 %collective-permute-start.39 = (bf16[256,1024]{1,0:T(8,128)(2,1)}, bf16[256,1024]{1,0:T(8,128)(2,1)S(1)}, u32[]{:S(2)}, u32[]{:S(2)}) collective-permute-start(bf16[256,1024]{1,0:T(8,128)(2,1)} %get-tuple-element.223.refs_13_), channel_id=1, source_target_pairs={{0,8},{8,16},{16,24},{24,28},{28,20},{20,12},{12,4},{4,0},{1,9},{9... | collective-permute-start | bytes 1572872 | tf_op jit(solution)/shard_map/ppermute | solution.py:812
  161.0 12.2 %collective-permute-start.40 = (bf16[256,1024]{1,0:T(8,128)(2,1)}, bf16[256,1024]{1,0:T(8,128)(2,1)S(1)}, u32[]{:S(2)}, u32[]{:S(2)}) collective-permute-start(bf16[256,1024]{1,0:T(8,128)(2,1)} %get-tuple-element.235), channel_id=1, source_target_pairs={{0,4},{8,0},{16,8},{24,16},{28,24},{20,28},{12,20},{4,12},{1,5},{9... | collective-permute-start | bytes 1572872 | tf_op jit(solution)/shard_map/ppermute | solution.py:812
  176.8 14.8 %collective-permute-start.41 = (bf16[256,1024]{1,0:T(8,128)(2,1)}, bf16[256,1024]{1,0:T(8,128)(2,1)S(1)}, u32[]{:S(2)}, u32[]{:S(2)}) collective-permute-start(bf16[256,1024]{1,0:T(8,128)(2,1)} %get-tuple-element.237.refs_16_), channel_id=1, source_target_pairs={{0,8},{8,16},{16,24},{24,28},{28,20},{20,12},{12,4},{4,0},{1,9},{9... | collective-permute-start | bytes 1572872 | tf_op jit(solution)/shard_map/ppermute | solution.py:812
  178.5 13.2 %collective-permute-start.42 = (bf16[256,1024]{1,0:T(8,128)(2,1)}, bf16[256,1024]{1,0:T(8,128)(2,1)S(1)}, u32[]{:S(2)}, u32[]{:S(2)}) collective-permute-start(bf16[256,1024]{1,0:T(8,128)(2,1)} %get-tuple-element.240), channel_id=1, source_target_pairs={{0,4},{8,0},{16,8},{24,16},{28,24},{20,28},{12,20},{4,12},{1,5},{9... | collective-permute-start | bytes 1572872 | tf_op jit(solution)/shard_map/ppermute | solution.py:812
  178.9 51.5 %collective-permute-start.60 = (bf16[2,128,1024]{2,1,0:T(8,128)(2,1)}, bf16[2,128,1024]{2,1,0:T(8,128)(2,1)S(1)}, u32[]{:S(2)}, u32[]{:S(2)}) collective-permute-start(bf16[2,128,1024]{2,1,0:T(8,128)(2,1)} %get-tuple-element.261), channel_id=1, source_target_pairs={{0,1},{1,0},{2,3},{3,2},{4,5},{5,4},{6,7},{7,6},{8,9},{9,8},{10,11... | collective-permute-start | bytes 1572872 | tf_op jit(solution)/shard_map/ppermute | solution.py:780
  204.2 14.2 %collective-permute-start.50 = (bf16[256,1024]{1,0:T(8,128)(2,1)}, bf16[256,1024]{1,0:T(8,128)(2,1)}, u32[]{:S(2)}, u32[]{:S(2)}) collective-permute-start(bf16[256,1024]{1,0:T(8,128)(2,1)} %constant_dynamic-update-slice_fusion.refs_2_), channel_id=1, source_target_pairs={{0,8},{8,16},{16,24},{24,28},{28,20},{20,12},{12,4},{4,0},{1,9},{9... | collective-permute-start | bytes 1572872 | tf_op jit(solution)/shard_map/ppermute | solution.py:812
  205.7 14.9 %collective-permute-start.51 = (bf16[256,1024]{1,0:T(8,128)(2,1)}, bf16[256,1024]{1,0:T(8,128)(2,1)S(1)}, u32[]{:S(2)}, u32[]{:S(2)}) collective-permute-start(bf16[256,1024]{1,0:T(8,128)(2,1)} %constant_dynamic-update-slice_fusion.refs_2_), channel_id=1, source_target_pairs={{0,4},{8,0},{16,8},{24,16},{28,24},{20,28},{12,20},{4,12},{1,5},{9... | collective-permute-start | bytes 1572872 | tf_op jit(solution)/shard_map/ppermute | solution.py:812
  221.4 22.7 %collective-permute-start.52 = (bf16[256,1024]{1,0:T(8,128)(2,1)}, bf16[256,1024]{1,0:T(8,128)(2,1)S(1)}, u32[]{:S(2)}, u32[]{:S(2)}) collective-permute-start(bf16[256,1024]{1,0:T(8,128)(2,1)} %shard_map.389.refs_3_), channel_id=1, source_target_pairs={{0,8},{8,16},{16,24},{24,28},{28,20},{20,12},{12,4},{4,0},{1,9},{9... | collective-permute-start | bytes 1572872 | tf_op jit(solution)/shard_map/ppermute | solution.py:812
  223.2 20.9 %collective-permute-start.53 = (bf16[256,1024]{1,0:T(8,128)(2,1)}, bf16[256,1024]{1,0:T(8,128)(2,1)S(1)}, u32[]{:S(2)}, u32[]{:S(2)}) collective-permute-start(bf16[256,1024]{1,0:T(8,128)(2,1)} %copy-done.48), channel_id=1, source_target_pairs={{0,4},{8,0},{16,8},{24,16},{28,24},{20,28},{12,20},{4,12},{1,5},{9... | collective-permute-start | bytes 1572872 | tf_op jit(solution)/shard_map/ppermute | solution.py:812
  223.8 29.6 %collective-permute-start.61 = (bf16[2,128,1024]{2,1,0:T(8,128)(2,1)S(1)}, bf16[2,128,1024]{2,1,0:T(8,128)(2,1)S(1)}, u32[]{:S(2)}, u32[]{:S(2)}) collective-permute-start(bf16[2,128,1024]{2,1,0:T(8,128)(2,1)S(1)} %copy-done.105), channel_id=1, source_target_pairs={{0,1},{1,0},{2,3},{3,2},{4,5},{5,4},{6,7},{7,6},{8,9},{9,8},{10,11... | collective-permute-start | bytes 1572872 | tf_op jit(solution)/shard_map/ppermute | solution.py:780
  228.6 15.1 %collective-permute-start.45 = (bf16[208,1024]{1,0:T(8,128)(2,1)}, bf16[208,1024]{1,0:T(8,128)(2,1)S(1)}, u32[]{:S(2)}, u32[]{:S(2)}) collective-permute-start(bf16[208,1024]{1,0:T(8,128)(2,1)} %get-tuple-element.251.refs_9_), channel_id=1, source_target_pairs={{0,8},{8,16},{16,24},{24,28},{28,20},{20,12},{12,4},{4,0},{1,9},{9... | collective-permute-start | bytes 1277960 | tf_op jit(solution)/shard_map/ppermute | solution.py:812
  230.4 13.7 %collective-permute-start.46 = (bf16[208,1024]{1,0:T(8,128)(2,1)}, bf16[208,1024]{1,0:T(8,128)(2,1)S(1)}, u32[]{:S(2)}, u32[]{:S(2)}) collective-permute-start(bf16[208,1024]{1,0:T(8,128)(2,1)} %get-tuple-element.252), channel_id=1, source_target_pairs={{0,4},{8,0},{16,8},{24,16},{28,24},{20,28},{12,20},{4,12},{1,5},{9... | collective-permute-start | bytes 1277960 | tf_op jit(solution)/shard_map/ppermute | solution.py:812
  249.3 13.0 %collective-permute-start.54 = (bf16[208,1024]{1,0:T(8,128)(2,1)}, bf16[208,1024]{1,0:T(8,128)(2,1)S(1)}, u32[]{:S(2)}, u32[]{:S(2)}) collective-permute-start(bf16[208,1024]{1,0:T(8,128)(2,1)} %get-tuple-element.256.refs_7_), channel_id=1, source_target_pairs={{0,8},{8,16},{16,24},{24,28},{28,20},{20,12},{12,4},{4,0},{1,9},{9... | collective-permute-start | bytes 1277960 | tf_op jit(solution)/shard_map/ppermute | solution.py:812
  250.9 13.0 %collective-permute-start.55 = (bf16[208,1024]{1,0:T(8,128)(2,1)}, bf16[208,1024]{1,0:T(8,128)(2,1)S(1)}, u32[]{:S(2)}, u32[]{:S(2)}) collective-permute-start(bf16[208,1024]{1,0:T(8,128)(2,1)} %get-tuple-element.257), channel_id=1, source_target_pairs={{0,4},{8,0},{16,8},{24,16},{28,24},{20,28},{12,20},{4,12},{1,5},{9... | collective-permute-start | bytes 1277960 | tf_op jit(solution)/shard_map/ppermute | solution.py:812
  251.4 22.2 %collective-permute-start.58 = (bf16[256,1024]{1,0:T(8,128)(2,1)}, bf16[256,1024]{1,0:T(8,128)(2,1)S(1)}, u32[]{:S(2)}, u32[]{:S(2)}) collective-permute-start(bf16[256,1024]{1,0:T(8,128)(2,1)} %copy-done.49), channel_id=1, source_target_pairs={{0,8},{8,16},{16,24},{24,28},{28,20},{20,12},{12,4},{4,0},{1,9},{9... | collective-permute-start | bytes 1572872 | tf_op jit(solution)/shard_map/ppermute | solution.py:812
  252.9 22.3 %collective-permute-start.59 = (bf16[256,1024]{1,0:T(8,128)(2,1)}, bf16[256,1024]{1,0:T(8,128)(2,1)S(1)}, u32[]{:S(2)}, u32[]{:S(2)}) collective-permute-start(bf16[256,1024]{1,0:T(8,128)(2,1)} %copy-done.50), channel_id=1, source_target_pairs={{0,4},{8,0},{16,8},{24,16},{28,24},{20,28},{12,20},{4,12},{1,5},{9... | collective-permute-start | bytes 1572872 | tf_op jit(solution)/shard_map/ppermute | solution.py:812
  253.6 22.2 %collective-permute-start.62 = (bf16[2,128,1024]{2,1,0:T(8,128)(2,1)S(1)}, bf16[2,128,1024]{2,1,0:T(8,128)(2,1)S(1)}, u32[]{:S(2)}, u32[]{:S(2)}) collective-permute-start(bf16[2,128,1024]{2,1,0:T(8,128)(2,1)S(1)} %pad_maximum_fusion.1), channel_id=1, source_target_pairs={{0,2},{1,3},{2,0},{3,1},{4,6},{5,7},{6,4},{7,5},{8,10},{9,11},{10,... | collective-permute-start | bytes 1572872 | tf_op jit(solution)/shard_map/ppermute | solution.py:780
  268.1 14.4 %collective-permute-start.56 = (bf16[208,1024]{1,0:T(8,128)(2,1)}, bf16[208,1024]{1,0:T(8,128)(2,1)S(1)}, u32[]{:S(2)}, u32[]{:S(2)}) collective-permute-start(bf16[208,1024]{1,0:T(8,128)(2,1)} %get-tuple-element.258.refs_11_), channel_id=1, source_target_pairs={{0,8},{8,16},{16,24},{24,28},{28,20},{20,12},{12,4},{4,0},{1,9},{9... | collective-permute-start | bytes 1277960 | tf_op jit(solution)/shard_map/ppermute | solution.py:812
  269.6 14.4 %collective-permute-start.57 = (bf16[208,1024]{1,0:T(8,128)(2,1)}, bf16[208,1024]{1,0:T(8,128)(2,1)S(1)}, u32[]{:S(2)}, u32[]{:S(2)}) collective-permute-start(bf16[208,1024]{1,0:T(8,128)(2,1)} %get-tuple-element.259), channel_id=1, source_target_pairs={{0,4},{8,0},{16,8},{24,16},{28,24},{20,28},{12,20},{4,12},{1,5},{9... | collective-permute-start | bytes 1277960 | tf_op jit(solution)/shard_map/ppermute | solution.py:812
  273.6 18.1 %collective-permute-start.63 = (bf16[128,1024]{1,0:T(8,128)(2,1)S(1)}, bf16[128,1024]{1,0:T(8,128)(2,1)S(1)}, u32[]{:S(2)}, u32[]{:S(2)}) collective-permute-start(bf16[128,1024]{1,0:T(8,128)(2,1)S(1)} %slice.40.refs_7_), channel_id=1, source_target_pairs={{0,8},{8,16},{16,24},{24,28},{28,20},{20,12},{12,4},{4,0},{1,9},{9... | collective-permute-start | bytes 786440 | tf_op jit(solution)/shard_map/ppermute | solution.py:812
  275.2 16.5 %collective-permute-start.64 = (bf16[128,1024]{1,0:T(8,128)(2,1)S(1)}, bf16[128,1024]{1,0:T(8,128)(2,1)S(1)}, u32[]{:S(2)}, u32[]{:S(2)}) collective-permute-start(bf16[128,1024]{1,0:T(8,128)(2,1)S(1)} %slice.41.refs_8_), channel_id=1, source_target_pairs={{0,4},{8,0},{16,8},{24,16},{28,24},{20,28},{12,20},{4,12},{1,5},{9... | collective-permute-start | bytes 786440 | tf_op jit(solution)/shard_map/ppermute | solution.py:812
  295.1 12.0 %collective-permute-start.68 = (bf16[208,1024]{1,0:T(8,128)(2,1)S(1)}, bf16[208,1024]{1,0:T(8,128)(2,1)S(1)}, u32[]{:S(2)}, u32[]{:S(2)}) collective-permute-start(bf16[208,1024]{1,0:T(8,128)(2,1)S(1)} %pad_maximum_fusion.2.refs_4_.refs_2_), channel_id=1, source_target_pairs={{0,8},{8,16},{16,24},{24,28},{28,20},{20,12},{12,4},{4,0},{1,9},{9... | collective-permute-start | bytes 1277960 | tf_op jit(solution)/shard_map/ppermute | solution.py:812
  296.7 11.7 %collective-permute-start.69 = (bf16[208,1024]{1,0:T(8,128)(2,1)S(1)}, bf16[208,1024]{1,0:T(8,128)(2,1)S(1)}, u32[]{:S(2)}, u32[]{:S(2)}) collective-permute-start(bf16[208,1024]{1,0:T(8,128)(2,1)S(1)} %pad_maximum_fusion.2.refs_4_.refs_2_), channel_id=1, source_target_pairs={{0,4},{8,0},{16,8},{24,16},{28,24},{20,28},{12,20},{4,12},{1,5},{9... | collective-permute-start | bytes 1277960 | tf_op jit(solution)/shard_map/ppermute | solution.py:812
  309.2 16.1 %collective-permute-start.70 = (bf16[2,2,128,1024]{3,2,1,0:T(8,128)(2,1)}, bf16[2,2,128,1024]{3,2,1,0:T(8,128)(2,1)S(1)}, u32[]{:S(2)}, u32[]{:S(2)}) collective-permute-start(bf16[2,2,128,1024]{3,2,1,0:T(8,128)(2,1)} %shard_map.397), channel_id=1, source_target_pairs={{0,1},{1,0},{2,3},{3,2},{4,5},{5,4},{6,7},{7,6},{8,9},{9,8},{10,11... | collective-permute-start | bytes 3145736 | tf_op jit(solution)/shard_map/ppermute | solution.py:780
  310.2 11.3 %collective-permute-start.72 = (bf16[208,1024]{1,0:T(8,128)(2,1)S(1)}, bf16[208,1024]{1,0:T(8,128)(2,1)S(1)}, u32[]{:S(2)}, u32[]{:S(2)}) collective-permute-start(bf16[208,1024]{1,0:T(8,128)(2,1)S(1)} %copy-done.4), channel_id=1, source_target_pairs={{0,8},{8,16},{16,24},{24,28},{28,20},{20,12},{12,4},{4,0},{1,9},{9... | collective-permute-start | bytes 1277960 | tf_op jit(solution)/shard_map/ppermute | solution.py:812
  311.5 11.0 %collective-permute-start.73 = (bf16[208,1024]{1,0:T(8,128)(2,1)S(1)}, bf16[208,1024]{1,0:T(8,128)(2,1)S(1)}, u32[]{:S(2)}, u32[]{:S(2)}) collective-permute-start(bf16[208,1024]{1,0:T(8,128)(2,1)S(1)} %copy-done.9), channel_id=1, source_target_pairs={{0,4},{8,0},{16,8},{24,16},{28,24},{20,28},{12,20},{4,12},{1,5},{9... | collective-permute-start | bytes 1277960 | tf_op jit(solution)/shard_map/ppermute | solution.py:812
  324.5 10.5 %collective-permute-start.75 = (bf16[208,1024]{1,0:T(8,128)(2,1)}, bf16[208,1024]{1,0:T(8,128)(2,1)S(1)}, u32[]{:S(2)}, u32[]{:S(2)}) collective-permute-start(bf16[208,1024]{1,0:T(8,128)(2,1)} %copy-done.10), channel_id=1, source_target_pairs={{0,4},{8,0},{16,8},{24,16},{28,24},{20,28},{12,20},{4,12},{1,5},{9... | collective-permute-start | bytes 1277960 | tf_op jit(solution)/shard_map/ppermute | solution.py:812
  325.5 11.7 %collective-permute-start.71 = (bf16[2,128,1024]{2,1,0:T(8,128)(2,1)S(1)}, bf16[2,128,1024]{2,1,0:T(8,128)(2,1)S(1)}, u32[]{:S(2)}, u32[]{:S(2)}) collective-permute-start(bf16[2,128,1024]{2,1,0:T(8,128)(2,1)S(1)} %fusion.3), channel_id=1, source_target_pairs={{0,2},{1,3},{2,0},{3,1},{4,6},{5,7},{6,4},{7,5},{8,10},{9,11},{10,... | collective-permute-start | bytes 1572872 | tf_op jit(solution)/shard_map/ppermute | solution.py:780
  (141 other events, 709.4 us)
